TPU v7x, 32 devices: a whole 2x2x4 slice. The times are simulated.
32 devices in a mesh: batch: 16 (over z, y, core), head: 2 (over x).
Axes of the slice: x: 2, y: 2, z: 4, core: 2. Of those that a mesh axis runs over, the one named last changes fastest.
Arguments:
- tokens: bfloat16 [14336, 1024], P('batch', 'head'), may hold values from -6 to 6
- ln_gain: float32 [1024], replicated, may hold values from 0.5 to 1.5
- w_qkv: bfloat16 [1024, 3072], P(None, 'head'), may hold values from -0.1875 to 0.1875
- qk_gain: float32 [2, 64], replicated, may hold values from 1 to 1.7
- w_out: bfloat16 [1024, 1024], P('head'), may hold values from -1 to 1
- w_up: bfloat16 [1024, 4096], P(None, 'head'), may hold values from -0.1875 to 0.1875
- b_up: float32 [4096], P('head'), may hold values from -3 to 3
- w_down: bfloat16 [4096, 1024], P('head'), may hold values from -0.09375 to 0.09375
- b_out: float32 [1024], P('head'), may hold values from -3 to 3
- cotangent: bfloat16 [14336, 1024], P('batch', 'head'), may hold values from -6 to 6
- slot_image: int32 [64], P('batch'), may hold values from 0 to 3, as said below
- token_valid: int32 [14336], P('batch'), may hold values from 0 to 1, as said below
Outputs:
- output: bfloat16 [14336, 1024], P('batch', 'head')
- grad_tokens: bfloat16 [14336, 1024], P('batch', 'head')
- grad_ln_gain: float32 [1024], P('head')
- grad_w_qkv: float32 [1024, 3072], P(None, 'head')
- grad_qk_gain: float32 [2, 64], replicated
- grad_w_out: float32 [1024, 1024], P('head')
- grad_w_up: float32 [1024, 4096], P(None, 'head')
- grad_b_up: float32 [4096], P('head')
- grad_w_down: float32 [4096, 1024], P('head')
- grad_b_out: float32 [1024], P('head')
Inputs may be any that keep to these rules, and one draw needn't show every extreme that they name: `slot_image`: within each group of 4 slots the image numbers start at 0, never fall, and rise by one from slot to slot, except that a long image takes the first 3 slots of some groups (at least one group in every draw); every other image takes one slot. `token_valid`: in each slot the valid rows come first; a long image has all of its 672 rows valid; a one-slot image has 112 to 196 valid rows, and the first one-slot image of every group has exactly 196.
All inputs are finite; a program needn't handle non-finite values.
Results may differ from a plain program's by a relative error of at most 0.012.
Values may be sent and summed in bfloat16 or wider, within the bound.
No kernel may reach another device: no remote copies, remote signals or barrier semaphores. Data moves between devices by JAX's collectives and lax.ppermute only.
A program may use at most 192 MiB of HBM per device.

v0:
```python
import functools

import jax
import jax.numpy as jnp
from jax import lax
from jax.experimental import pallas as pl
from jax.experimental.pallas import tpu as pltpu
from jax.sharding import PartitionSpec as P

HD = 64
EPSILON = 1e-06
FAR = -16384.0
LOW = jnp.bfloat16
WIDE = jnp.float32
MIB = 1024 * 1024
SHORT = pl.CostEstimate(flops=1024, bytes_accessed=1024, transcendentals=0)


def contract(left, right, left_dim, right_dim):
    return lax.dot_general(
        left, right, (((left_dim,), (right_dim,)), ((), ())), preferred_element_type=WIDE
    )


def swap(values, axis):
    return lax.ppermute(values, axis, [(0, 1), (1, 0)])


def both_halves(mine, other, first, dim):
    return jnp.where(
        first,
        jnp.concatenate([mine, other], axis=dim),
        jnp.concatenate([other, mine], axis=dim),
    )


def mlp_body(normed_ref, w_ref, b_ref, hidden_ref, slope_ref):
    pre = jnp.dot(normed_ref[...], w_ref[...], preferred_element_type=WIDE) + b_ref[...]
    cdf = 0.5 * (1.0 + lax.erf(pre * (0.5**0.5)))
    density = jnp.exp(-0.5 * pre * pre) * 0.3989422804014327
    hidden_ref[...] = (pre * cdf).astype(LOW)
    slope_ref[...] = (cdf + pre * density).astype(LOW)


def streamed(values):
    return pltpu.with_memory_space_constraint(values, pltpu.HBM)


def mlp_forward(normed, w_up, b_up):
    rows, width = normed.shape
    units = w_up.shape[1]
    block = 512
    return pl.pallas_call(
        mlp_body,
        grid=(units // block,),
        in_specs=[
            pl.BlockSpec((rows, width), lambda i: (0, 0)),
            pl.BlockSpec((width, block), lambda i: (0, i)),
            pl.BlockSpec((1, block), lambda i: (0, i)),
        ],
        out_specs=[
            pl.BlockSpec((rows, block), lambda i: (0, i)),
            pl.BlockSpec((rows, block), lambda i: (0, i)),
        ],
        out_shape=[
            jax.ShapeDtypeStruct((rows, units), LOW),
            jax.ShapeDtypeStruct((rows, units), LOW),
        ],
        compiler_params=pltpu.CompilerParams(vmem_limit_bytes=16 * MIB),
        cost_estimate=SHORT,
        name="mlp_forward",
    )(normed, streamed(w_up), b_up.reshape(1, units))


def norm_body(side_ref, mine_ref, other_ref, gain_ref, normed_ref, stats_ref):
    mine = mine_ref[...].astype(WIDE)
    other = other_ref[...].astype(WIDE)
    width = 2 * mine.shape[1]
    half = mine.shape[1]
    center = (
        jnp.sum(mine, axis=1, keepdims=True) + jnp.sum(other, axis=1, keepdims=True)
    ) / width
    mine = mine - center
    other = other - center
    spread = (
        jnp.sum(mine * mine, axis=1, keepdims=True)
        + jnp.sum(other * other, axis=1, keepdims=True)
    ) / width
    scaled = lax.rsqrt(spread + EPSILON)
    first = side_ref[0] == 0
    left = jnp.where(first, mine, other)
    right = jnp.where(first, other, mine)
    normed_ref[:, 0:half] = (left * scaled * gain_ref[:, 0:half]).astype(LOW)
    normed_ref[:, half:width] = (right * scaled * gain_ref[:, half:width]).astype(LOW)
    lane = lax.broadcasted_iota(jnp.int32, stats_ref.shape, 1)
    stats_ref[...] = jnp.where(lane == 0, center, scaled)


def input_norm(side, mine, other, gain):
    rows, half = mine.shape
    block = 224
    return pl.pallas_call(
        norm_body,
        grid_spec=pltpu.PrefetchScalarGridSpec(
            num_scalar_prefetch=1,
            grid=(rows // block,),
            in_specs=[
                pl.BlockSpec((block, half), lambda i, s: (i, 0)),
                pl.BlockSpec((block, half), lambda i, s: (i, 0)),
                pl.BlockSpec((1, 2 * half), lambda i, s: (0, 0)),
            ],
            out_specs=[
                pl.BlockSpec((block, 2 * half), lambda i, s: (i, 0)),
                pl.BlockSpec((block, 128), lambda i, s: (i, 0)),
            ],
        ),
        out_shape=[
            jax.ShapeDtypeStruct((rows, 2 * half), LOW),
            jax.ShapeDtypeStruct((rows, 128), WIDE),
        ],
        cost_estimate=SHORT,
        name="input_norm",
    )(side, mine, other, gain.reshape(1, 2 * half))


def slope_body(side_ref, mine_ref, other_ref, w_ref, slope_ref, grad_pre_ref, bias_ref, piece_ref):
    half = mine_ref.shape[1]

    @pl.when(pl.program_id(0) == 0)
    def _():
        first = side_ref[0] == 0
        mine, other = mine_ref[...], other_ref[...]
        piece_ref[:, 0:half] = jnp.where(first, mine, other)
        piece_ref[:, half:] = jnp.where(first, other, mine)

    back = lax.dot_general(
        piece_ref[...], w_ref[...], (((1,), (1,)), ((), ())), preferred_element_type=WIDE
    )
    low = (back * slope_ref[...].astype(WIDE)).astype(LOW)
    grad_pre_ref[...] = low
    bias_ref[...] = jnp.sum(low.astype(WIDE), axis=0, keepdims=True)


def mlp_slope(side, mine, other, w_down, slope):
    rows, half = mine.shape
    units, width = w_down.shape
    block = 512

    def whole(i, s):
        return (0, 0)

    return pl.pallas_call(
        slope_body,
        grid_spec=pltpu.PrefetchScalarGridSpec(
            num_scalar_prefetch=1,
            grid=(units // block,),
            in_specs=[
                pl.BlockSpec((rows, half), whole),
                pl.BlockSpec((rows, half), whole),
                pl.BlockSpec((block, width), lambda i, s: (i, 0)),
                pl.BlockSpec((rows, block), lambda i, s: (0, i)),
            ],
            out_specs=[
                pl.BlockSpec((rows, block), lambda i, s: (0, i)),
                pl.BlockSpec((1, block), lambda i, s: (0, i)),
                pl.BlockSpec((rows, width), whole),
            ],
        ),
        out_shape=[
            jax.ShapeDtypeStruct((rows, units), LOW),
            jax.ShapeDtypeStruct((1, units), WIDE),
            jax.ShapeDtypeStruct((rows, width), LOW),
        ],
        compiler_params=pltpu.CompilerParams(vmem_limit_bytes=20 * MIB),
        cost_estimate=SHORT,
        name="mlp_slope",
    )(side, mine, other, streamed(w_down), slope)


def first_dims(left, right):
    return lax.dot_general(left, right, (((0,), (0,)), ((), ())), preferred_element_type=WIDE)


def mlp_weights_body(down_steps, hidden_ref, piece_ref, normed_ref, grad_pre_ref, *refs):
    step = pl.program_id(0)
    out_ref = refs[-1]

    def put(total):
        if len(refs) == 2:
            total = total + refs[0][...].astype(WIDE)
        out_ref[...] = total.astype(LOW)

    @pl.when(step < down_steps)
    def _():
        put(first_dims(hidden_ref[...], piece_ref[...]))

    @pl.when(step >= down_steps)
    def _():
        put(first_dims(normed_ref[...], grad_pre_ref[...]))


def mlp_weights(hidden, piece, normed, grad_pre, *before):
    rows, units = hidden.shape
    width = piece.shape[1]
    block = 512
    down = units // block
    across = width // block
    halves = units // width

    def later(i):
        return jnp.maximum(i - down, 0)

    return pl.pallas_call(
        functools.partial(mlp_weights_body, down),
        grid=(down + halves * across,),
        in_specs=[
            pl.BlockSpec((rows, block), lambda i: (0, jnp.minimum(i, down - 1))),
            pl.BlockSpec((rows, width), lambda i: (0, 0)),
            pl.BlockSpec((rows, block), lambda i: (0, later(i) % across)),
            pl.BlockSpec((rows, width), lambda i: (0, later(i) // across)),
        ]
        + [pl.BlockSpec((block, width), lambda i: (i, 0)) for _ in before],
        out_specs=pl.BlockSpec((block, width), lambda i: (i, 0)),
        out_shape=pltpu.HBM((2 * units, width), LOW),
        input_output_aliases={4: 0} if before else {},
        compiler_params=pltpu.CompilerParams(vmem_limit_bytes=24 * MIB),
        cost_estimate=SHORT,
        name="mlp_weights",
    )(hidden, piece, normed, grad_pre, *before)


def heads_weights_body(steps, normed_ref, piece_ref, grad_joined_ref, attended_ref, out_ref):
    width = out_ref.shape[1]
    rest = grad_joined_ref.shape[1] - width

    block = out_ref.shape[0]
    lines = pl.ds(pl.multiple_of(pl.program_id(0) % steps * block, block), block)

    @pl.when(pl.program_id(0) < steps)
    def _():
        out_ref[...] = first_dims(normed_ref[:, lines], grad_joined_ref[:, 0:width]).astype(LOW)

    @pl.when(pl.program_id(0) >= steps)
    def _():
        out_ref[:, 0:rest] = first_dims(
            normed_ref[:, lines], grad_joined_ref[:, width:]
        ).astype(LOW)
        out_ref[:, rest:] = lax.dot_general(
            piece_ref[:, lines], attended_ref[...], (((0,), (1,)), ((), ())), preferred_element_type=WIDE
        ).astype(LOW)


def heads_weights(normed, grad_joined, piece, attended_t):
    rows, width = normed.shape
    block = 512
    steps = width // block
    return pl.pallas_call(
        functools.partial(heads_weights_body, steps),
        grid=(2 * steps,),
        in_specs=[
            pl.BlockSpec(normed.shape, lambda i: (0, 0)),
            pl.BlockSpec(piece.shape, lambda i: (0, 0)),
            pl.BlockSpec(grad_joined.shape, lambda i: (0, 0)),
            pl.BlockSpec(attended_t.shape, lambda i: (0, 0)),
        ],
        out_specs=pl.BlockSpec((block, width), lambda i: (i, 0)),
        out_shape=pltpu.HBM((2 * width, width), LOW),
        compiler_params=pltpu.CompilerParams(vmem_limit_bytes=20 * MIB),
        cost_estimate=SHORT,
        name="heads_weights",
    )(normed, piece, grad_joined, attended_t)


def spread_body(mlp_ref, left_ref, right_ref, down_ref, up_ref, qkv_ref, out_ref):
    step = pl.program_id(0)
    steps = pl.num_programs(0)

    @pl.when(step < steps // 2)
    def _():
        down_ref[...] = mlp_ref[...].astype(WIDE).reshape(down_ref.shape)

    @pl.when(step >= steps // 2)
    def _():
        up_ref[...] = mlp_ref[...].astype(WIDE).reshape(up_ref.shape)

    lines, columns = qkv_ref.shape
    width = left_ref.shape[-1]
    qkv_ref[:, 0:width] = left_ref[...].astype(WIDE).reshape(lines, width)
    right = right_ref[...].astype(WIDE).reshape(lines, width)
    qkv_ref[:, width:columns] = right[:, 0 : columns - width]
    out_ref[...] = jnp.transpose(right[:, columns - width :])


def spread(whole, n, units, columns):
    width = whole.shape[1]
    mlp_rows, heads_rows = 2 * units // n, 2 * width // n
    assert whole.shape[0] == n * (mlp_rows + heads_rows) and mlp_rows % heads_rows == 0
    steps = width // 128
    block = 2 * units // steps
    inner = 2 * width - columns
    across = width // block
    skip = mlp_rows // heads_rows

    def later(i):
        return jnp.maximum(i - steps // 2, 0)

    by_rows = streamed(whole.reshape(n, -1, width))
    by_parts = streamed(whole.reshape(n, -1, heads_rows, width))
    part = (n // (2 * steps), 1, heads_rows, width)
    return pl.pallas_call(
        spread_body,
        grid=(steps,),
        in_specs=[
            pl.BlockSpec((n // steps, mlp_rows, width), lambda i: (i, 0, 0)),
            pl.BlockSpec(part, lambda i: (i, skip, 0, 0)),
            pl.BlockSpec(part, lambda i: (i + steps, skip, 0, 0)),
        ],
        out_specs=[
            pl.BlockSpec((block, width), lambda i: (jnp.minimum(i, steps // 2 - 1), 0)),
            pl.BlockSpec((block, width), lambda i: (later(i) % across, later(i) // across)),
            pl.BlockSpec((128, columns), lambda i: (i, 0)),
            pl.BlockSpec((inner, 128), lambda i: (0, i)),
        ],
        out_shape=[
            jax.ShapeDtypeStruct((units, width), WIDE),
            jax.ShapeDtypeStruct((width, units), WIDE),
            jax.ShapeDtypeStruct((width, columns), WIDE),
            jax.ShapeDtypeStruct((inner, width), WIDE),
        ],
        compiler_params=pltpu.CompilerParams(vmem_limit_bytes=32 * MIB),
        cost_estimate=SHORT,
        name="spread",
    )(by_rows, by_parts, by_parts)


def output_body(count, side_ref, w_out_ref, hidden_ref, w_down_ref, *refs):
    attended_refs, (away_ref, kept_ref) = refs[:count], refs[count:]
    step = pl.program_id(0)
    attended = jnp.concatenate([ref[...] for ref in attended_refs], axis=0)
    total = jnp.dot(
        hidden_ref[...], w_down_ref[...], preferred_element_type=WIDE
    ) + first_dims(attended, w_out_ref[...])

    @pl.when(step == 0)
    def _():
        away_ref[...] = total.astype(LOW)

    @pl.when(step == 1)
    def _():
        kept_ref[...] = total


def output_terms(side, w_out, hidden, w_down, attended_t):
    rows, units = hidden.shape
    inner, width = w_out.shape
    half = width // 2

    def column(i, s):
        return (0, s[0] ^ (1 - i))

    def whole(i, s):
        return (0, 0)

    return pl.pallas_call(
        functools.partial(output_body, len(attended_t)),
        grid_spec=pltpu.PrefetchScalarGridSpec(
            num_scalar_prefetch=1,
            grid=(2,),
            in_specs=[
                pl.BlockSpec((inner, half), column),
                pl.BlockSpec((rows, units), whole),
                pl.BlockSpec((units, half), column),
            ]
            + [pl.BlockSpec(v.shape, whole) for v in attended_t],
            out_specs=[pl.BlockSpec((rows, half), whole)] * 2,
        ),
        out_shape=[
            jax.ShapeDtypeStruct((rows, half), LOW),
            jax.ShapeDtypeStruct((rows, half), WIDE),
        ],
        compiler_params=pltpu.CompilerParams(vmem_limit_bytes=24 * MIB),
        cost_estimate=SHORT,
        name="output_terms",
    )(side, w_out, hidden, w_down, *attended_t)


def second_dims(left, right):
    return lax.dot_general(left, right, (((1,), (1,)), ((), ())), preferred_element_type=WIDE)


def grad_in_body(count, side_ref, w_qkv_ref, grad_pre_ref, w_up_ref, *refs):
    away_ref, kept_ref = refs[count:]
    step = pl.program_id(0)
    grad_joined = jnp.concatenate([ref[...] for ref in refs[:count]], axis=1)
    total = second_dims(grad_joined, w_qkv_ref[...]) + second_dims(
        grad_pre_ref[...], w_up_ref[...]
    )

    @pl.when(step == 0)
    def _():
        away_ref[...] = total.astype(LOW)

    @pl.when(step == 1)
    def _():
        kept_ref[...] = total


def grad_in_terms(side, w_qkv, grad_pre, w_up, grad_joined):
    rows, units = grad_pre.shape
    width, columns = w_qkv.shape
    half = width // 2

    def picked(i, s):
        return (s[0] ^ (1 - i), 0)

    def whole(i, s):
        return (0, 0)

    return pl.pallas_call(
        functools.partial(grad_in_body, len(grad_joined)),
        grid_spec=pltpu.PrefetchScalarGridSpec(
            num_scalar_prefetch=1,
            grid=(2,),
            in_specs=[
                pl.BlockSpec((half, columns), picked),
                pl.BlockSpec((rows, units), whole),
                pl.BlockSpec((half, units), picked),
            ]
            + [pl.BlockSpec(v.shape, whole) for v in grad_joined],
            out_specs=[pl.BlockSpec((rows, half), whole)] * 2,
        ),
        out_shape=[
            jax.ShapeDtypeStruct((rows, half), LOW),
            jax.ShapeDtypeStruct((rows, half), WIDE),
        ],
        compiler_params=pltpu.CompilerParams(vmem_limit_bytes=24 * MIB),
        cost_estimate=SHORT,
        name="grad_in_terms",
    )(side, streamed(w_qkv), grad_pre, streamed(w_up), *grad_joined)


def hat_body(side_ref, kept_ref, arrived_ref, tokens_ref, stats_ref, gain_ref,
             hat_ref, sums_ref, gain_grad_ref):
    total = kept_ref[...] + arrived_ref[...].astype(WIDE)
    stats = stats_ref[...]
    x_hat = (tokens_ref[...].astype(WIDE) - stats[:, 0:1]) * stats[:, 1:2]
    grad_hat = total * gain_ref[...]
    hat_ref[...] = grad_hat
    lane = lax.broadcasted_iota(jnp.int32, stats.shape, 1)
    sums_ref[...] = jnp.where(
        lane == 0,
        jnp.sum(grad_hat, axis=1, keepdims=True),
        jnp.sum(grad_hat * x_hat, axis=1, keepdims=True),
    )

    @pl.when(pl.program_id(0) == 0)
    def _():
        gain_grad_ref[...] = jnp.zeros_like(gain_grad_ref)

    gain_grad_ref[...] += jnp.sum(total * x_hat, axis=0, keepdims=True)


def grad_in_hat(side, kept, arrived, tokens, stats, gain):
    rows, half = tokens.shape
    block = 448

    def rows_of(columns):
        return pl.BlockSpec((block, columns), lambda i, s: (i, 0))

    return pl.pallas_call(
        hat_body,
        grid_spec=pltpu.PrefetchScalarGridSpec(
            num_scalar_prefetch=1,
            grid=(rows // block,),
            in_specs=[rows_of(half), rows_of(half), rows_of(half), rows_of(128),
                      pl.BlockSpec((1, half), lambda i, s: (0, s[0]))],
            out_specs=[rows_of(half), rows_of(128), pl.BlockSpec((1, half), lambda i, s: (0, 0))],
        ),
        out_shape=[
            jax.ShapeDtypeStruct((rows, half), WIDE),
            jax.ShapeDtypeStruct((rows, 128), WIDE),
            jax.ShapeDtypeStruct((1, half), WIDE),
        ],
        cost_estimate=SHORT,
        name="grad_in_hat",
    )(side, kept, arrived, tokens, stats, gain)


def finish_body(cotangent_ref, tokens_ref, stats_ref, hat_ref, sums_ref, other_ref, out_ref):
    width = 2 * tokens_ref.shape[1]
    scaled = stats_ref[:, 1:2]
    x_hat = (tokens_ref[...].astype(WIDE) - stats_ref[:, 0:1]) * scaled
    sums = (sums_ref[:, 0:2] + other_ref[...]) / width
    out_ref[...] = (
        cotangent_ref[...].astype(WIDE)
        + scaled * (hat_ref[...] - sums[:, 0:1] - x_hat * sums[:, 1:2])
    ).astype(LOW)


def grad_in_finish(cotangent, tokens, stats, hat, sums, other):
    rows, half = tokens.shape
    block = 224

    def rows_of(columns):
        return pl.BlockSpec((block, columns), lambda i: (i, 0))

    return pl.pallas_call(
        finish_body,
        grid=(rows // block,),
        in_specs=[rows_of(c) for c in (half, half, 128, half, 128, 2)],
        out_specs=rows_of(half),
        out_shape=jax.ShapeDtypeStruct((rows, half), LOW),
        cost_estimate=SHORT,
        name="grad_in_finish",
    )(cotangent, tokens, stats, hat, sums, other)


def part_norm(values):
    center = jnp.mean(values, axis=0, keepdims=True)
    shifted = values - center
    scaled = lax.rsqrt(jnp.mean(shifted * shifted, axis=0, keepdims=True) + EPSILON)
    return shifted * scaled, scaled


def part_norm_back(grad, normal, scaled, gain):
    g = grad * gain
    inner = jnp.mean(g * normal, axis=0, keepdims=True)
    return scaled * (g - jnp.mean(g, axis=0, keepdims=True) - normal * inner)


def lane_fold(values):
    total = values[:, 0:128]
    for start in range(128, values.shape[1], 128):
        total = total + values[:, start : start + 128]
    return total


def attention_body(rows, tiles, count, *refs):
    joined_refs, grad_refs = refs[:count], refs[count : 2 * count]
    (gain_ref, query_mark_ref, key_mark_ref, attended_ref, grad_joined_ref, gain_grad_ref,
     key_grad, value_grad) = refs[2 * count :]

    def part(some, r0, r1):
        return jnp.concatenate([ref[r0:r1, :] for ref in some], axis=1)

    factor = float(HD) ** (-0.5)
    gain_query = gain_ref[0:HD, :]
    gain_key = gain_ref[HD : 2 * HD, :]
    pieces = []
    gain_sum_query = jnp.zeros((HD, 128), WIDE)
    gain_sum_key = jnp.zeros((HD, 128), WIDE)
    one_mark = jnp.where(lax.broadcasted_iota(jnp.int32, (HD, rows), 0) < 2, 1.0, 0.0).astype(LOW)
    for head in range(2):
        base = head * 3 * HD
        query_hat, query_scale = part_norm(part(joined_refs, base, base + HD))
        key_hat, key_scale = part_norm(part(joined_refs, base + HD, base + 2 * HD))
        value_t = part(joined_refs, base + 2 * HD, base + 3 * HD).astype(LOW)
        query_t = (query_hat * gain_query).astype(LOW)
        key_t = (key_hat * gain_key).astype(LOW)
        grad_t = part(grad_refs, head * HD, (head + 1) * HD)
        query_aug = jnp.concatenate([query_t * factor, query_mark_ref[...]], axis=0)
        key_aug = jnp.transpose(jnp.concatenate([key_t, key_mark_ref[...]], axis=0))
        value_aug_t = jnp.concatenate([value_t, one_mark], axis=0)
        value_aug = jnp.transpose(value_aug_t)
        query_grads = []
        for number, (q0, q1, k0, k1) in enumerate(tiles):
            scores = jnp.dot(key_aug[k0:k1], query_aug[:, q0:q1], preferred_element_type=WIDE)
            terms = jnp.exp(scores)
            terms_low = terms.astype(LOW)
            summed = jnp.dot(value_aug_t[:, k0:k1], terms_low, preferred_element_type=WIDE)
            inverse = 1.0 / summed[HD : HD + 1, :]
            attended = summed[0:HD, :] * inverse
            attended_ref[head * HD : (head + 1) * HD, q0:q1] = attended.astype(LOW)
            grad_tile = grad_t[:, q0:q1].astype(WIDE)
            row_inner = jnp.sum(grad_tile * attended, axis=0, keepdims=True)
            inner_high = row_inner.astype(LOW)
            inner_low = (row_inner - inner_high.astype(WIDE)).astype(LOW)
            place = lax.broadcasted_iota(jnp.int32, (HD, q1 - q0), 0)
            inner_mark = jnp.where(
                place == 0,
                -inner_high.astype(WIDE),
                jnp.where(place == 1, -inner_low.astype(WIDE), 0.0),
            ).astype(LOW)
            grad_aug = jnp.concatenate([grad_t[:, q0:q1], inner_mark], axis=0)
            shifted = jnp.dot(value_aug[k0:k1], grad_aug, preferred_element_type=WIDE)
            grad_scores = (terms * shifted).astype(LOW)
            query_grads.append(
                jnp.dot(key_t[:, k0:k1], grad_scores, preferred_element_type=WIDE)
                * (inverse * factor)
            )
            query_rows = jnp.transpose(
                jnp.concatenate(
                    [query_t[:, q0:q1].astype(WIDE) * (inverse * factor), grad_tile * inverse],
                    axis=0,
                ).astype(LOW)
            )
            key_term = jnp.dot(grad_scores, query_rows, preferred_element_type=WIDE)
            value_term = jnp.dot(terms_low, query_rows, preferred_element_type=WIDE)
            if number == 0:
                key_grad[k0:k1, :] = key_term
                value_grad[k0:k1, :] = value_term
                key_grad[k1:rows, :] = jnp.zeros((rows - k1, 2 * HD), WIDE)
                value_grad[k1:rows, :] = jnp.zeros((rows - k1, 2 * HD), WIDE)
            else:
                key_grad[k0:k1, :] += key_term
                value_grad[k0:k1, :] += value_term
        lane = lax.broadcasted_iota(jnp.int32, (rows, 2 * HD), 1)
        joint = jnp.transpose(jnp.where(lane < HD, key_grad[...], value_grad[...]))
        query_grad = jnp.concatenate(query_grads, axis=1)
        key_grad_t = joint[0:HD, :]
        gain_sum_query += lane_fold(query_grad * query_hat)
        gain_sum_key += lane_fold(key_grad_t * key_hat)
        pieces += [
            part_norm_back(query_grad, query_hat, query_scale, gain_query),
            part_norm_back(key_grad_t, key_hat, key_scale, gain_key),
            joint[HD : 2 * HD, :],
        ]
    grad_joined_ref[...] = jnp.transpose(jnp.concatenate(pieces, axis=0)).astype(LOW)

    @pl.when(pl.program_id(0) == 0)
    def _():
        gain_grad_ref[...] = jnp.zeros_like(gain_grad_ref)

    gain_grad_ref[...] += jnp.concatenate([gain_sum_query, gain_sum_key], axis=0)


def attention(joined_t, grad_t, gains, query_mark, key_mark, skip, pairs):
    rows = query_mark.shape[1]
    heads = 2 * pairs
    width = heads * 3 * HD
    far = 3 * (rows // 4)
    tiles = ((0, 512, 0, far), (512, 768, 0, rows), (768, rows, far, rows))

    def whole(i):
        return (0, 0)

    return pl.pallas_call(
        functools.partial(attention_body, rows, tiles, len(joined_t)),
        grid=(heads // 2,),
        in_specs=[pl.BlockSpec((6 * HD, v.shape[1]), lambda i: (i + skip, 0)) for v in joined_t]
        + [pl.BlockSpec((2 * HD, v.shape[1]), lambda i: (i + skip, 0)) for v in grad_t]
        + [
            pl.BlockSpec((2 * HD, 1), whole),
            pl.BlockSpec((HD, rows), whole),
            pl.BlockSpec((HD, rows), whole),
        ],
        out_specs=[
            pl.BlockSpec((2 * HD, rows), lambda i: (i, 0)),
            pl.BlockSpec((rows, 6 * HD), lambda i: (0, i)),
            pl.BlockSpec((2 * HD, 128), whole),
        ],
        out_shape=[
            jax.ShapeDtypeStruct((heads * HD, rows), LOW),
            jax.ShapeDtypeStruct((rows, width), LOW),
            jax.ShapeDtypeStruct((2 * HD, 128), WIDE),
        ],
        scratch_shapes=[
            pltpu.VMEM((rows, 2 * HD), WIDE),
            pltpu.VMEM((rows, 2 * HD), WIDE),
        ],
        compiler_params=pltpu.CompilerParams(vmem_limit_bytes=20 * MIB),
        cost_estimate=SHORT,
        name="attention_both",
    )(*joined_t, *grad_t, gains, query_mark, key_mark)


def ring_order(n):
    if n % 4:
        return list(range(n))
    up = [z * 4 + c for z in range(n // 4) for c in range(2)]
    down = [z * 4 + 2 + c for z in reversed(range(n // 4)) for c in range(2)]
    return up + down


def ring_scatter(values, n):
    return lax.psum_scatter(
        values, "batch", scatter_dimension=0, tiled=True, axis_index_groups=[ring_order(n)]
    )


def chips_scatter(values, n):
    order = ring_order(n)
    groups = [order[0::2], order[1::2]]
    return lax.psum_scatter(
        values, "batch", scatter_dimension=0, tiled=True, axis_index_groups=groups
    )


def ring_gather(own, n):
    return lax.all_gather(own, "batch", axis=0, tiled=True, axis_index_groups=[ring_order(n)])


def send(values, pairs):
    return lax.ppermute(values, "batch", pairs)


def exchange(values, bit, n):
    return send(values, [(i, i ^ bit) for i in range(n)])


def added(left, right):
    return (left.astype(WIDE) + right.astype(WIDE)).astype(LOW)


def then(done, *values):
    return lax.optimization_barrier((done, values))[1]


def ring_view(values, n):
    bits = max(n.bit_length() - 3, 0)
    return values.reshape((2,) + (2,) * bits + (2, values.shape[0] // n, values.shape[1]))


def ring_half(bit, place, n):
    dims = n.bit_length()
    mine = (place // bit) % 2
    if bit == 1:
        return dims - 2, mine
    if bit == 2:
        return 0, mine
    return dims - 1 - bit.bit_length() + 1, mine ^ ((place // 2) % 2)


def pair_send(values, bit, place, n):
    dim, mine = ring_half(bit, place, n)
    return exchange(lax.dynamic_slice_in_dim(values, 1 - mine, 1, dim), bit, n)


def pair_add(values, arrived, bit, place, n):
    dim, mine = ring_half(bit, place, n)
    return added(lax.dynamic_slice_in_dim(values, mine, 1, dim), arrived)


def pair_join(mine, other, bit, place, n):
    dim, half = ring_half(bit, place, n)
    return both_halves(mine, other, half == 0, dim)


def line_place(place, n):
    count = n // 4
    up = place // 4
    return jnp.where((place // 2) % 2 == 0, up, count - 1 - up), count


def line_send(values, place, n):
    mine, count = line_place(place, n)
    blocks = values.reshape(count, values.size // count // values.shape[-1], values.shape[-1])
    return blocks, [
        exchange(lax.dynamic_index_in_dim(blocks, mine ^ k, 0, False), 4 * k, n)
        for k in range(1, count)
    ]


def line_add(blocks, arrived, place, n):
    mine, _ = line_place(place, n)
    total = lax.dynamic_index_in_dim(blocks, mine, 0, False).astype(WIDE)
    for values in arrived:
        total = total + values.astype(WIDE)
    return total.astype(LOW)


def small_sums(values, n, afters):
    bit = 1
    while bit < n:
        bits = (bit, 2 * bit, 3 * bit) if bit * 4 <= n else (bit,)
        moved = [exchange(values, b, n) for b in bits]
        if afters:
            moved = then(afters.pop(0), *moved)
        values = values + moved[0]
        if len(bits) == 3:
            values = values + (moved[1] + moved[2])
        bit *= 4
    return values


def on_device(n_batch, tokens, ln_gain, w_qkv, qk_gain, w_out, w_up, b_up, w_down, b_out,
              cotangent, slot_image, token_valid):
    rows, half = tokens.shape
    width = 2 * half
    slots = slot_image.shape[0]
    slot_rows = rows // slots
    side = lax.axis_index("head")
    first = side == 0
    place = lax.axis_index("batch")
    sides = jnp.reshape(side, (1,)).astype(jnp.int32)
    bits = []
    while 4 * 2 ** len(bits) < n_batch:
        bits.append(4 * 2 ** len(bits))

    other_tokens = swap(tokens, "head")
    (held,) = then(tokens, cotangent)
    other_cotangent = swap(held, "head")

    token_image = jnp.repeat(slot_image, slot_rows, total_repeat_length=rows)
    ids = lax.broadcasted_iota(jnp.int32, (HD, rows), 0)
    same = token_image[None, :] == ids
    query_mark = jnp.where(same, 1.0, 0.0).astype(LOW)
    key_mark = jnp.where(same & (token_valid == 1)[None, :], 0.0, FAR)
    key_mark = jnp.where(ids < slots, key_mark, 0.0).astype(LOW)
    gains = qk_gain.reshape(-1, 1)
    grad_b_out = jnp.sum(cotangent.astype(WIDE), axis=0)
    (query_mark, key_mark, gains, grad_b_out), other_tokens = lax.optimization_barrier(
        ((query_mark, key_mark, gains, grad_b_out), other_tokens)
    )

    normed, stats = input_norm(sides, tokens, other_tokens, ln_gain)
    hidden, slope = mlp_forward(normed, w_up, b_up)
    grad_pre, grad_b_up, piece = mlp_slope(sides, cotangent, other_cotangent, w_down, slope)
    mlp_part = mlp_weights(hidden, piece, normed, grad_pre)
    mlp_own = ring_scatter(mlp_part, n_batch)

    def sent(part, bit):
        return pair_send(part, bit, place, n_batch)

    def summed(after, part, arrived, bit):
        (arrived,) = then(after, arrived)
        return pair_add(part, arrived, bit, place, n_batch)

    part, some = then(mlp_part, piece, normed)
    joined_t = contract(w_qkv, some, 0, 1)
    grad_t = contract(w_out, part, 1, 1).astype(LOW)
    marks = (gains, query_mark, key_mark)
    pairs = w_out.shape[0] // (2 * HD)
    joined_t, grad_t = then((joined_t, grad_t), joined_t, grad_t)
    attended, grad_joined, gain_grad = attention([joined_t], [grad_t], *marks, 0, pairs)
    heads_part = heads_weights(normed, grad_joined, piece, attended)
    heads_part = ring_view(heads_part, n_batch)
    branch = (sides, w_out, hidden, w_down, [attended])
    back = (sides, w_qkv, grad_pre, w_up, [grad_joined])
    way = sent(heads_part, 1)
    heads_part = summed(heads_part, heads_part, way, 1)
    mlp_own, heads_part = then(heads_part, mlp_own, heads_part)
    heads_own = chips_scatter(heads_part.reshape(-1, width), n_batch)
    mlp_rows = mlp_own.shape[0]
    away_in, kept_in = grad_in_terms(*then(mlp_own, *back))
    arrived_in = swap(away_in, "head")
    (mlp_own,) = then(away_in, mlp_own)
    own = lax.dynamic_update_slice(
        jnp.zeros((mlp_rows + 2 * width // n_batch, width), LOW), mlp_own, (0, 0)
    )
    away_out, kept_out = output_terms(*then(away_in, *branch))
    arrived_out = swap(away_out, "head")
    own, heads_own = then((away_out, arrived_in), own, heads_own)
    own = lax.dynamic_update_slice(own, heads_own, (mlp_rows, 0))
    whole = ring_gather(own, n_batch)

    (arrived_in,) = then(own, arrived_in)
    hat, sums, grad_ln = grad_in_hat(
        sides, kept_in, arrived_in, tokens, stats, ln_gain.reshape(1, width)
    )
    gain_grad = jnp.sum(gain_grad, axis=1).reshape(2, HD)
    joint = jnp.concatenate([sums[:, 0:2].T, gain_grad], axis=1)
    joint_other = swap(joint, "head")
    (joint_other,) = then(hat, joint_other)
    sums_other = joint_other[:, 0:rows].T
    gain_grad = (gain_grad + joint_other[:, rows:]).reshape(-1)
    small = jnp.concatenate([grad_ln[0], grad_b_out, grad_b_up[0], gain_grad])
    grad_tokens = grad_in_finish(cotangent, tokens, stats, hat, sums, sums_other)
    (arrived_out,) = then(grad_tokens, arrived_out)
    output = (
        tokens.astype(WIDE) + (kept_out + arrived_out.astype(WIDE)) + b_out
    ).astype(LOW)
    small = small_sums(small, n_batch, [grad_tokens, output])
    units = b_up.shape[0]
    (whole,) = then((output, grad_tokens, small), whole)
    grad_wd, grad_wup, grad_wqkv, grad_wo = spread(whole, n_batch, units, w_qkv.shape[1])
    return (
        output,
        grad_tokens,
        small[0:half],
        grad_wqkv,
        small[2 * half + units :].reshape(qk_gain.shape),
        grad_wo,
        grad_wup,
        small[2 * half : 2 * half + units],
        grad_wd,
        small[half : 2 * half],
    )


def solution(mesh):
    placed = (
        P("batch", "head"),
        P(),
        P(None, "head"),
        P(),
        P("head", None),
        P(None, "head"),
        P("head"),
        P("head", None),
        P("head"),
        P("batch", "head"),
        P("batch"),
        P("batch"),
    )
    return jax.shard_map(
        functools.partial(on_device, mesh.shape["batch"]),
        mesh=mesh,
        in_specs=placed,
        out_specs=(
            P("batch", "head"),
            P("batch", "head"),
            P("head"),
            P(None, "head"),
            P(),
            P("head", None),
            P(None, "head"),
            P("head"),
            P("head", None),
            P("head"),
        ),
        check_vma=False,
    )
```

profile of v0, /device:TPU:0, one launch (start us, length us, event | category | flops | bytes accessed | tf_op | source)
XLA Modules:
  0.0 261.2 jit_solution(6900714782599001845)
XLA Ops:
  7.2 3.0 %collective-permute-start = (bf16[896,512]{1,0:T(8,128)(2,1)}, bf16[896,512]{1,0:T(8,128)(2,1)S(1)}, u32[]{:S(2)}, u32[]{:S(2)}) collective-permute-start(bf16[896,512]{1,0:T(8,128)(2,1)} %tokens_ref.3), channel_id=1, source_target_pairs={{0,1},{1,0},{2,3},{3,2},{4,5},{5,4},{6,7},{7,6},{8,9},{9,8},{10,11... | collective-permute-start | bytes 2752520 | tf_op jit(solution)/shard_map/ppermute | solution.py:26
  10.2 0.1 collective-permute-start.1
  10.3 0.8 reshape.151
  11.1 1.4 fusion.3
  12.5 1.4 convert_reduce_fusion
  13.8 0.7 broadcast_compare_fusion
  14.5 3.3 %select_select_fusion = s32[896]{0:T(1024)S(1)} fusion(pred[896]{0:T(1024)(128)(4,1)} %constant.158, pred[896]{0:T(1024)(128)(4,1)} %constant.159, pred[896]{0:T(1024)(128)(4,1)} %constant.160, s32[]{:T(128)} %bitcast.4, s32[]{:T(128)} %bitcast.1, s32[]{:T(128)} %bitcast.2, s32[]{:T(128)} %bitcast.3), kind=kLoop, calls=%fused_computation.17 | loop fusion | flops 2688 | bytes 6288 | tf_op jit(solution)/shard_map/jit(_take)/gather | solution.py:794
  17.8 0.1 select_convert_fusion
  17.9 13.7 %collective-permute-done.other_ref = bf16[896,512]{1,0:T(8,128)(2,1)S(1)} collective-permute-done((bf16[896,512]{1,0:T(8,128)(2,1)}, bf16[896,512]{1,0:T(8,128)(2,1)S(1)}, u32[]{:S(2)}, u32[]{:S(2)}) %collective-permute-start) | collective-permute-done | bytes 917536 | tf_op jit(solution)/shard_map/ppermute | solution.py:26
  31.6 0.9 copy-done.19
  32.6 4.6 %input_norm.1 = (bf16[896,1024]{1,0:T(8,128)(2,1)}, f32[896,128]{1,0:T(8,128)}) custom-call(s32[1]{0:T(128)} %bitcast.side_ref, bf16[896,512]{1,0:T(8,128)(2,1)} %tokens_ref.3, bf16[896,512]{1,0:T(8,128)(2,1)} %copy-done.19, f32[1,1024]{1,0:T(1,128)} %bitcast.34), custom_call_target="tpu_custom_call" | custom-call | flops 1024 | bytes 1024 | tf_op jit(solution)/shard_map/input_norm/pallas_call | solution.py:102
  37.1 1.5 copy-done.1
  38.6 8.8 %mlp_forward.1 = (bf16[896,2048]{1,0:T(8,128)(2,1)S(1)}, bf16[896,2048]{1,0:T(8,128)(2,1)S(1)}) custom-call(bf16[896,1024]{1,0:T(8,128)(2,1)S(1)} %copy-done.1, bf16[1024,2048]{1,0:T(8,128)(2,1)} %w_up_ref, f32[1,2048]{1,0:T(1,128)S(1)} %bitcast.27), custom_call_target="tpu_custom_call" | custom-call | flops 1024 | bytes 1024 | tf_op jit(solution)/shard_map/mlp_forward/pallas_call | solution.py:53
  47.4 3.1 %collective-permute-done.1.other_ref = bf16[896,512]{1,0:T(8,128)(2,1)S(1)} collective-permute-done((bf16[896,512]{1,0:T(8,128)(2,1)}, bf16[896,512]{1,0:T(8,128)(2,1)S(1)}, u32[]{:S(2)}, u32[]{:S(2)}) %collective-permute-start.1) | collective-permute-done | bytes 917536 | tf_op jit(solution)/shard_map/ppermute | solution.py:26
  50.5 6.9 %mlp_slope.1 = (bf16[896,2048]{1,0:T(8,128)(2,1)S(1)}, f32[1,2048]{1,0:T(1,128)S(1)}, bf16[896,1024]{1,0:T(8,128)(2,1)S(1)}) custom-call(s32[1]{0:T(128)} %bitcast.side_ref, bf16[896,512]{1,0:T(8,128)(2,1)S(1)} %copy-done.9, bf16[896,512]{1,0:T(8,128)(2,1)S(1)} %collective-permute-done.1.other_ref, bf16[2048,1024]{1,0:T(8,128)(2,1)} %w_down_ref, ...), custom_call_target="tpu_custom_call" | custom-call | flops 1024 | bytes 1024 | tf_op jit(solution)/shard_map/mlp_slope/pallas_call | solution.py:152
  57.4 12.3 %mlp_weights.1 = bf16[4096,1024]{1,0:T(8,128)(2,1)} custom-call(bf16[896,2048]{1,0:T(8,128)(2,1)S(1)} %get-tuple-element.105.hidden_ref, bf16[896,1024]{1,0:T(8,128)(2,1)S(1)} %get-tuple-element.87.piece_ref, bf16[896,1024]{1,0:T(8,128)(2,1)S(1)} %copy-done.2, bf16[896,2048]{1,0:T(8,128)(2,1)S(1)} %get-tuple-element.99.grad_pre_ref), custom_call_target="tpu_custom_call" | custom-call | flops 1024 | bytes 1024 | tf_op jit(solution)/shard_map/mlp_weights/pallas_call | solution.py:213
  69.7 1.8 copy-done.5
  71.5 1.2 copy-done.10
  72.8 0.1 copy.43.refs_2_
  72.9 1.0 copy-done.15
  74.0 2.9 %fusion.refs_1_ = bf16[512,896]{1,0:T(8,128)(2,1)S(1)} fusion(bf16[896,1024]{1,0:T(8,128)(2,1)} %copy-done.10, bf16[512,1024]{1,0:T(8,128)(2,1)S(1)} %copy-done.15), kind=kOutput, calls=%fused_computation.5 | convolution fusion | flops 939982848 | bytes 3801088 | tf_op jit(solution)/shard_map/dot_general | solution.py:20
  76.9 3.5 %convolution_bitcast_fusion.refs_0_ = f32[1536,896]{1,0:T(8,128)S(1)} fusion(bf16[896,1024]{1,0:T(8,128)(2,1)S(1)} %copy-done.2, bf16[1024,1536]{1,0:T(8,128)(2,1)S(1)} %copy-done.18), kind=kOutput, calls=%fused_computation.1 | convolution fusion | flops 2818572288 | bytes 10485760 | tf_op jit(solution)/shard_map/dot_general | solution.py:20
  80.4 25.6 %attention_both.1 = (bf16[512,896]{1,0:T(8,128)(2,1)S(1)}, bf16[896,1536]{1,0:T(8,128)(2,1)S(1)}, f32[128,128]{1,0:T(8,128)S(1)}) custom-call(f32[1536,896]{1,0:T(8,128)S(1)} %convolution_bitcast_fusion.refs_0_, bf16[512,896]{1,0:T(8,128)(2,1)S(1)} %fusion.refs_1_, f32[128,1]{1,0:T(8,128)S(1)} %copy.43.refs_2_, ...), custom_call_target="tpu_custom_call" | custom-call | flops 1024 | bytes 1024 | tf_op jit(solution)/shard_map/attention_both/pallas_call | solution.py:637
  106.1 6.2 %heads_weights.1 = bf16[2048,1024]{1,0:T(8,128)(2,1)} custom-call(bf16[896,1024]{1,0:T(8,128)(2,1)S(1)} %copy-done.2, bf16[896,1024]{1,0:T(8,128)(2,1)S(1)} %copy-done.11, bf16[896,1536]{1,0:T(8,128)(2,1)S(1)} %get-tuple-element.101.grad_joined_ref.refs_0_, bf16[512,896]{1,0:T(8,128)(2,1)S(1)} %get-tuple-element.107.attended_ref.refs_0_), custom_call_target="tpu_custom_call" | custom-call | flops 1024 | bytes 1024 | tf_op jit(solution)/shard_map/heads_weights/pallas_call | solution.py:257
  112.3 1.9 constant_dynamic-slice_fusion
  114.2 0.1 collective-permute-start.2
  114.3 4.3 %collective-permute-done.2 = bf16[2,2,2,1,128,1024]{5,4,3,2,1,0:T(8,128)(2,1)} collective-permute-done((bf16[2,2,2,1,128,1024]{5,4,3,2,1,0:T(8,128)(2,1)S(1)}, bf16[2,2,2,1,128,1024]{5,4,3,2,1,0:T(8,128)(2,1)}, u32[]{:S(2)}, u32[]{:S(2)}) %collective-permute-start.2) | collective-permute-done | bytes 2097184 | tf_op jit(solution)/shard_map/ppermute | solution.py:694
  118.6 4.9 %add_convert_fusion = bf16[2,2,2,1,128,1024]{5,4,3,2,1,0:T(8,128)(2,1)} fusion(bf16[2,2,2,1,128,1024]{5,4,3,2,1,0:T(8,128)(2,1)} %collective-permute-done.2, bf16[2,2,2,2,128,1024]{5,4,3,2,1,0:T(8,128)(2,1)} %bitcast.32, s32[]{:T(128)S(6)} %select_n.57), kind=kLoop, calls=%fused_computation | loop fusion | flops 4194304 | bytes 6291460 | tf_op jit(solution)/shard_map/convert_element_type | solution.py:702
  123.4 9.1 %reduce-scatter.3.cloned.1.call-done = bf16[256,1024]{1,0:T(8,128)(2,1)} async-done(((bf16[4096,1024]{1,0:T(8,128)(2,1)}), bf16[256,1024]{1,0:T(8,128)(2,1)}) %reduce-scatter.3.cloned.1.call-update) | async-done | bytes 524304 | tf_op jit(solution)/shard_map/reduce_scatter | solution.py:676
  132.6 2.0 copy-done.6
  134.6 9.7 %grad_in_terms.1 = (bf16[896,512]{1,0:T(8,128)(2,1)S(1)}, f32[896,512]{1,0:T(8,128)S(1)}) custom-call(s32[1]{0:T(128)} %bitcast.side_ref, bf16[1024,1536]{1,0:T(8,128)(2,1)} %w_qkv_ref, bf16[896,2048]{1,0:T(8,128)(2,1)S(1)} %copy-done.6, bf16[1024,2048]{1,0:T(8,128)(2,1)} %w_up_ref, bf16[896,1536]{1,0:T(8,128)(2,1)S(1)} %copy-done.8), custom_call_target="tpu_custom_call" | custom-call | flops 1024 | bytes 1024 | tf_op jit(solution)/shard_map/grad_in_terms/pallas_call | solution.py:419
  144.4 1.2 copy-done.14
  145.6 0.9 collective-permute-start.3
  146.5 5.8 %output_terms.1 = (bf16[896,512]{1,0:T(8,128)(2,1)S(1)}, f32[896,512]{1,0:T(8,128)S(1)}) custom-call(s32[1]{0:T(128)} %bitcast.side_ref, bf16[512,1024]{1,0:T(8,128)(2,1)S(1)} %copy-done.16, bf16[896,2048]{1,0:T(8,128)(2,1)S(1)} %copy-done.4, bf16[2048,1024]{1,0:T(8,128)(2,1)S(1)} %copy-done, bf16[512,896]{1,0:T(8,128)(2,1)S(1)} %copy-done.13), custom_call_target="tpu_custom_call" | custom-call | flops 1024 | bytes 1024 | tf_op jit(solution)/shard_map/output_terms/pallas_call | solution.py:364
  152.3 1.0 dynamic_update_slice.6
  153.2 14.9 %collective-permute-done.3.arrived_ref = bf16[896,512]{1,0:T(8,128)(2,1)} collective-permute-done((bf16[896,512]{1,0:T(8,128)(2,1)S(1)}, bf16[896,512]{1,0:T(8,128)(2,1)}, u32[]{:S(2)}, u32[]{:S(2)}) %collective-permute-start.3) | collective-permute-done | bytes 917536 | tf_op jit(solution)/shard_map/ppermute | solution.py:26
  168.1 0.1 reduce-scatter.5.cloned.1.call-done
  168.2 1.7 constant_dynamic-update-slice_fusion
  169.9 0.1 reduce_sum.19
  170.0 0.1 reshape.156
  170.1 0.1 copy.44
  170.2 1.6 collective-permute-start.5
  171.8 3.6 %grad_in_hat.1 = (f32[896,512]{1,0:T(8,128)}, f32[896,128]{1,0:T(8,128)}, f32[1,512]{1,0:T(1,128)}) custom-call(s32[1]{0:T(128)} %bitcast.side_ref, f32[896,512]{1,0:T(8,128)} %copy-done.14, bf16[896,512]{1,0:T(8,128)(2,1)} %collective-permute-done.3.arrived_ref, bf16[896,512]{1,0:T(8,128)(2,1)} %tokens_ref.3, f32[896,128]{1,0:T(8,128)} %get-tuple-element.109.stats_ref, ...), custom_call_target="tpu_custom_call" | custom-call | flops 1024 | bytes 1024 | tf_op jit(solution)/shard_map/grad_in_hat/pallas_call | solution.py:470
  175.4 1.1 slice_bitcast_fusion.1
  176.6 0.5 collective-permute-start.4
  177.0 25.3 %collective-permute-done.4 = f32[2,960]{0,1:T(8,128)S(1)} collective-permute-done((f32[2,960]{0,1:T(8,128)S(1)}, f32[2,960]{0,1:T(8,128)S(1)}, u32[]{:S(2)}, u32[]{:S(2)}) %collective-permute-start.4) | collective-permute-done | bytes 7712 | tf_op jit(solution)/shard_map/ppermute | solution.py:26
  202.3 0.8 copy-done.21
  203.1 0.1 copy.46
  203.2 0.1 reshape.157
  203.3 0.7 pad_maximum_fusion.1
  204.0 0.7 collective-permute-start.7
  204.7 1.1 collective-permute-start.6
  205.8 1.8 slice_bitcast_fusion.other_ref
  207.7 4.7 %grad_in_finish.1 = bf16[896,512]{1,0:T(8,128)(2,1)} custom-call(bf16[896,512]{1,0:T(8,128)(2,1)} %cotangent_ref.1, bf16[896,512]{1,0:T(8,128)(2,1)} %tokens_ref.3, f32[896,128]{1,0:T(8,128)} %get-tuple-element.109.stats_ref, f32[896,512]{1,0:T(8,128)} %get-tuple-element.117.hat_ref, f32[896,128]{1,0:T(8,128)} %get-tuple-element.118.sums_ref, ...), custom_call_target="tpu_custom_call" | custom-call | flops 1024 | bytes 1024 | tf_op jit(solution)/shard_map/grad_in_finish/pallas_call | solution.py:507
  212.4 3.4 %collective-permute-start.11 = (f32[3200]{0:T(1024)S(1)}, f32[3200]{0:T(1024)S(1)}, u32[]{:S(2)}, u32[]{:S(2)}) collective-permute-start(f32[3200]{0:T(1024)S(1)} %add_add_fusion.1), channel_id=1, source_target_pairs={{0,24},{2,26},{4,28},{6,30},{8,16},{10,18},{12,20},{14,22},{16,8},... | collective-permute-start | bytes 38408 | tf_op jit(solution)/shard_map/ppermute | solution.py:694
  215.8 0.4 collective-permute-start.10
  216.2 0.6 collective-permute-start.9
  216.8 2.8 %add_convert_fusion.1 = bf16[896,512]{1,0:T(8,128)(2,1)} fusion(f32[896,512]{1,0:T(8,128)S(1)} %get-tuple-element.108, bf16[896,512]{1,0:T(8,128)(2,1)} %collective-permute-done.5, bf16[896,512]{1,0:T(8,128)(2,1)} %tokens_ref.3, f32[512]{0:T(512)S(1)} %copy-done.23), kind=kLoop, calls=%fused_computation.2 | loop fusion | flops 2752512 | bytes 4589568 | tf_op jit(solution)/shard_map/convert_element_type | solution.py:862
  219.7 1.1 collective-permute-done.10
  220.8 0.6 slice.62
  221.4 0.6 slice.52
  222.1 0.6 fusion.2
  222.7 17.5 %all-gather.2.cloned.1.call-done = bf16[6144,1024]{1,0:T(8,128)(2,1)} async-done(((bf16[384,1024]{1,0:T(8,128)(2,1)}), bf16[6144,1024]{1,0:T(8,128)(2,1)}) %all-gather.2.cloned.1.call-update) | async-done | bytes 12582928 | tf_op jit(solution)/shard_map/all_gather | solution.py:690
  240.2 14.5 %spread.1 = (f32[2048,1024]{1,0:T(8,128)}, f32[1024,2048]{1,0:T(8,128)}, f32[1024,1536]{1,0:T(8,128)}, f32[512,1024]{1,0:T(8,128)}) custom-call(bf16[16,384,1024]{2,1,0:T(8,128)(2,1)} %bitcast.28, bf16[16,3,128,1024]{3,2,1,0:T(8,128)(2,1)} %bitcast.29, bf16[16,3,128,1024]{3,2,1,0:T(8,128)(2,1)} %bitcast.30), custom_call_target="tpu_custom_call" | custom-call | flops 1024 | bytes 1024 | tf_op jit(solution)/shard_map/spread/pallas_call | solution.py:310
  (59 shorter events, 0.3 us)
Async XLA Ops:
  7.2 29.9 %copy-start.17 = (f32[2048]{0:T(1024)S(1)}, f32[2048]{0:T(1024)}, u32[]{:S(2)}) copy-start(f32[2048]{0:T(1024)} %param.20) | copy-start | bytes 24580
  7.2 125.3 %reduce-scatter.3.cloned.1.call-start = ((), (), s32[]{:S(2)}) async-start(), calls=%async_computation.2 | async-start | bytes 8912896 | tf_op jit(solution)/shard_map/reduce_scatter | solution.py:676
  7.2 24.4 %collective-permute-start = (bf16[896,512]{1,0:T(8,128)(2,1)}, bf16[896,512]{1,0:T(8,128)(2,1)S(1)}, u32[]{:S(2)}, u32[]{:S(2)}) collective-permute-start(bf16[896,512]{1,0:T(8,128)(2,1)} %tokens_ref.3), channel_id=1, source_target_pairs={{0,1},{1,0},{2,3},{3,2},{4,5},{5,4},{6,7},{7,6},{8,9},{9,8},{10,11... | collective-permute-start | bytes 2752520 | tf_op jit(solution)/shard_map/ppermute | solution.py:26
  10.2 40.2 %collective-permute-start.1 = (bf16[896,512]{1,0:T(8,128)(2,1)}, bf16[896,512]{1,0:T(8,128)(2,1)S(1)}, u32[]{:S(2)}, u32[]{:S(2)}) collective-permute-start(bf16[896,512]{1,0:T(8,128)(2,1)} %cotangent_ref.1), channel_id=1, source_target_pairs={{0,1},{1,0},{2,3},{3,2},{4,5},{5,4},{6,7},{7,6},{8,9},{9,8},{10,11... | collective-permute-start | bytes 2752520 | tf_op jit(solution)/shard_map/ppermute | solution.py:26
  31.6 0.9 copy-start.19
  37.1 1.5 copy-start.1
  38.6 11.8 %copy-start.9 = (bf16[896,512]{1,0:T(8,128)(2,1)S(1)}, bf16[896,512]{1,0:T(8,128)(2,1)}, u32[]{:S(2)}) copy-start(bf16[896,512]{1,0:T(8,128)(2,1)} %cotangent_ref.1) | copy-start | bytes 2752516
  47.4 10.0 %copy-start.3 = (bf16[896,2048]{1,0:T(8,128)(2,1)}, bf16[896,2048]{1,0:T(8,128)(2,1)S(1)}, u32[]{:S(2)}) copy-start(bf16[896,2048]{1,0:T(8,128)(2,1)S(1)} %get-tuple-element.105.hidden_ref) | copy-start | bytes 11010052
  50.5 6.9 %copy-start.2 = (bf16[896,1024]{1,0:T(8,128)(2,1)S(1)}, bf16[896,1024]{1,0:T(8,128)(2,1)}, u32[]{:S(2)}) copy-start(bf16[896,1024]{1,0:T(8,128)(2,1)} %get-tuple-element.86.normed_ref) | copy-start | bytes 5505028
  69.7 1.8 copy-start.5
  71.5 1.2 copy-start.10
  72.7 1.2 copy-start.15
  72.7 95.5 %reduce-scatter.5.cloned.1.call-start = ((), (), s32[]{:S(2)}) async-start(), calls=%async_computation.3 | async-start | bytes 2359296 | tf_op jit(solution)/shard_map/reduce_scatter | solution.py:684
  73.9 2.9 %copy-start.18 = (bf16[1024,1536]{1,0:T(8,128)(2,1)S(1)}, bf16[1024,1536]{1,0:T(8,128)(2,1)}, u32[]{:S(2)}) copy-start(bf16[1024,1536]{1,0:T(8,128)(2,1)} %w_qkv_ref) | copy-start | bytes 9437188
  80.4 25.7 %copy-start.11 = (bf16[896,1024]{1,0:T(8,128)(2,1)S(1)}, bf16[896,1024]{1,0:T(8,128)(2,1)}, u32[]{:S(2)}) copy-start(bf16[896,1024]{1,0:T(8,128)(2,1)} %copy-done.10) | copy-start | bytes 5505028
  106.0 6.2 %copy-start.7 = (bf16[896,1536]{1,0:T(8,128)(2,1)}, bf16[896,1536]{1,0:T(8,128)(2,1)S(1)}, u32[]{:S(2)}) copy-start(bf16[896,1536]{1,0:T(8,128)(2,1)S(1)} %get-tuple-element.101.grad_joined_ref.refs_0_) | copy-start | bytes 8257540
  106.0 6.2 %copy-start.12 = (bf16[512,896]{1,0:T(8,128)(2,1)}, bf16[512,896]{1,0:T(8,128)(2,1)S(1)}, u32[]{:S(2)}) copy-start(bf16[512,896]{1,0:T(8,128)(2,1)S(1)} %get-tuple-element.107.attended_ref.refs_0_) | copy-start | bytes 2752516
  114.2 4.4 %collective-permute-start.2 = (bf16[2,2,2,1,128,1024]{5,4,3,2,1,0:T(8,128)(2,1)S(1)}, bf16[2,2,2,1,128,1024]{5,4,3,2,1,0:T(8,128)(2,1)}, u32[]{:S(2)}, u32[]{:S(2)}) collective-permute-start(bf16[2,2,2,1,128,1024]{5,4,3,2,1,0:T(8,128)(2,1)S(1)} %constant_dynamic-slice_fusion), channel_id=1, source_target_pairs={{0,2},{2,0},{4,6},{6,4},{8,10},{10,8},{12,14},{14,12},{16,18},{18,... | collective-permute-start | bytes 6291464 | tf_op jit(solution)/shard_map/ppermute | solution.py:694
  118.6 14.0 %copy-start.8 = (bf16[896,1536]{1,0:T(8,128)(2,1)S(1)}, bf16[896,1536]{1,0:T(8,128)(2,1)}, u32[]{:S(2)}) copy-start(bf16[896,1536]{1,0:T(8,128)(2,1)} %copy-done.7) | copy-start | bytes 8257540
  132.5 107.7 %all-gather.2.cloned.1.call-start = ((), (), s32[]{:S(2)}) async-start(), calls=%async_computation.4 | async-start | bytes 13369344 | tf_op jit(solution)/shard_map/all_gather | solution.py:690
  132.6 2.0 copy-start.6
  134.6 11.8 %copy-start = (bf16[2048,1024]{1,0:T(8,128)(2,1)S(1)}, bf16[2048,1024]{1,0:T(8,128)(2,1)}, u32[]{:S(2)}) copy-start(bf16[2048,1024]{1,0:T(8,128)(2,1)} %w_down_ref) | copy-start | bytes 12582916
  134.6 11.8 %copy-start.4 = (bf16[896,2048]{1,0:T(8,128)(2,1)S(1)}, bf16[896,2048]{1,0:T(8,128)(2,1)}, u32[]{:S(2)}) copy-start(bf16[896,2048]{1,0:T(8,128)(2,1)} %copy-done.3) | copy-start | bytes 11010052
  134.6 11.8 %copy-start.13 = (bf16[512,896]{1,0:T(8,128)(2,1)S(1)}, bf16[512,896]{1,0:T(8,128)(2,1)}, u32[]{:S(2)}) copy-start(bf16[512,896]{1,0:T(8,128)(2,1)} %copy-done.12) | copy-start | bytes 2752516
  134.6 11.8 %copy-start.16 = (bf16[512,1024]{1,0:T(8,128)(2,1)S(1)}, bf16[512,1024]{1,0:T(8,128)(2,1)}, u32[]{:S(2)}) copy-start(bf16[512,1024]{1,0:T(8,128)(2,1)} %w_out_ref) | copy-start | bytes 3145732
  144.3 1.2 copy-start.14
  145.6 6.7 %copy-start.20 = (bf16[256,1024]{1,0:T(8,128)(2,1)S(1)}, bf16[256,1024]{1,0:T(8,128)(2,1)}, u32[]{:S(2)}) copy-start(bf16[256,1024]{1,0:T(8,128)(2,1)} %reduce-scatter.3.cloned.1.call-done) | copy-start | bytes 1572868
  145.6 22.6 %collective-permute-start.3 = (bf16[896,512]{1,0:T(8,128)(2,1)S(1)}, bf16[896,512]{1,0:T(8,128)(2,1)}, u32[]{:S(2)}, u32[]{:S(2)}) collective-permute-start(bf16[896,512]{1,0:T(8,128)(2,1)S(1)} %get-tuple-element.102), channel_id=1, source_target_pairs={{0,1},{1,0},{2,3},{3,2},{4,5},{5,4},{6,7},{7,6},{8,9},{9,8},{10,11... | collective-permute-start | bytes 2752520 | tf_op jit(solution)/shard_map/ppermute | solution.py:26
  170.2 42.1 %collective-permute-start.5 = (bf16[896,512]{1,0:T(8,128)(2,1)S(1)}, bf16[896,512]{1,0:T(8,128)(2,1)}, u32[]{:S(2)}, u32[]{:S(2)}) collective-permute-start(bf16[896,512]{1,0:T(8,128)(2,1)S(1)} %get-tuple-element.111), channel_id=1, source_target_pairs={{0,1},{1,0},{2,3},{3,2},{4,5},{5,4},{6,7},{7,6},{8,9},{9,8},{10,11... | collective-permute-start | bytes 2752520 | tf_op jit(solution)/shard_map/ppermute | solution.py:26
  176.6 25.8 %collective-permute-start.4 = (f32[2,960]{0,1:T(8,128)S(1)}, f32[2,960]{0,1:T(8,128)S(1)}, u32[]{:S(2)}, u32[]{:S(2)}) collective-permute-start(f32[2,960]{0,1:T(8,128)S(1)} %pad_maximum_fusion), channel_id=1, source_target_pairs={{0,1},{1,0},{2,3},{3,2},{4,5},{5,4},{6,7},{7,6},{8,9},{9,8},{10,11... | collective-permute-start | bytes 23048 | tf_op jit(solution)/shard_map/ppermute | solution.py:26
  202.3 0.8 copy-start.21
  204.0 8.3 %collective-permute-start.8 = (f32[3200]{0:T(1024)S(1)}, f32[3200]{0:T(1024)S(1)}, u32[]{:S(2)}, u32[]{:S(2)}) collective-permute-start(f32[3200]{0:T(1024)S(1)} %pad_maximum_fusion.1), channel_id=1, source_target_pairs={{0,6},{2,4},{4,2},{6,0},{8,14},{10,12},{12,10},{14,8},{16,22},{18,... | collective-permute-start | bytes 38408 | tf_op jit(solution)/shard_map/ppermute | solution.py:694
  204.0 8.3 %collective-permute-start.7 = (f32[3200]{0:T(1024)S(1)}, f32[3200]{0:T(1024)S(1)}, u32[]{:S(2)}, u32[]{:S(2)}) collective-permute-start(f32[3200]{0:T(1024)S(1)} %pad_maximum_fusion.1), channel_id=1, source_target_pairs={{0,4},{2,6},{4,0},{6,2},{8,12},{10,14},{12,8},{14,10},{16,20},{18,... | collective-permute-start | bytes 38408 | tf_op jit(solution)/shard_map/ppermute | solution.py:694
  204.7 7.6 %collective-permute-start.6 = (f32[3200]{0:T(1024)S(1)}, f32[3200]{0:T(1024)S(1)}, u32[]{:S(2)}, u32[]{:S(2)}) collective-permute-start(f32[3200]{0:T(1024)S(1)} %pad_maximum_fusion.1), channel_id=1, source_target_pairs={{0,2},{2,0},{4,6},{6,4},{8,10},{10,8},{12,14},{14,12},{16,18},{18,... | collective-permute-start | bytes 38408 | tf_op jit(solution)/shard_map/ppermute | solution.py:694
  207.7 4.7 %copy-start.22 = (f32[1,512]{1,0:T(1,128)S(1)}, f32[1,512]{1,0:T(1,128)}, u32[]{:S(2)}) copy-start(f32[1,512]{1,0:T(1,128)} %get-tuple-element.122) | copy-start | bytes 6148
  207.7 9.2 %copy-start.23 = (f32[512]{0:T(512)S(1)}, f32[512]{0:T(512)}, u32[]{:S(2)}) copy-start(f32[512]{0:T(512)} %param.22) | copy-start | bytes 6148
  212.4 7.3 %collective-permute-start.11 = (f32[3200]{0:T(1024)S(1)}, f32[3200]{0:T(1024)S(1)}, u32[]{:S(2)}, u32[]{:S(2)}) collective-permute-start(f32[3200]{0:T(1024)S(1)} %add_add_fusion.1), channel_id=1, source_target_pairs={{0,24},{2,26},{4,28},{6,30},{8,16},{10,18},{12,20},{14,22},{16,8},... | collective-permute-start | bytes 38408 | tf_op jit(solution)/shard_map/ppermute | solution.py:694
  215.8 5.1 %collective-permute-start.10 = (f32[3200]{0:T(1024)S(1)}, f32[3200]{0:T(1024)S(1)}, u32[]{:S(2)}, u32[]{:S(2)}) collective-permute-start(f32[3200]{0:T(1024)S(1)} %add_add_fusion.1), channel_id=1, source_target_pairs={{0,16},{2,18},{4,20},{6,22},{8,24},{10,26},{12,28},{14,30},{16,0},... | collective-permute-start | bytes 38408 | tf_op jit(solution)/shard_map/ppermute | solution.py:694
  216.2 4.6 %collective-permute-start.9 = (f32[3200]{0:T(1024)S(1)}, f32[3200]{0:T(1024)S(1)}, u32[]{:S(2)}, u32[]{:S(2)}) collective-permute-start(f32[3200]{0:T(1024)S(1)} %add_add_fusion.1), channel_id=1, source_target_pairs={{0,8},{2,10},{4,12},{6,14},{8,0},{10,2},{12,4},{14,6},{16,24},{18,... | collective-permute-start | bytes 38408 | tf_op jit(solution)/shard_map/ppermute | solution.py:694
Sparse Core Ops, SparseCore 0:
  72.9 59.5 reduce-scatter.2
  135.4 32.8 reduce-scatter.4
  170.4 69.7 all-gather.1
where the time goes:
time: 262 us; the launch traced here: 261 us
  Pallas kernels  103 us (39%)
  waiting for transfers between devices  89.2 us (34%)
  local copies, waits for them, and re-layouts  22.5 us (9%)
  between operations  14.1 us (5%)
  other arithmetic  14 us (5%)
  starting transfers between devices  12.5 us (5%)
  matrix products  6.4 us (2%)
    ppermute x5, waiting for transfers between devices, swap(): return lax.ppermute(values, axis, [(0, 1), (1, 0)])  57 us
    pallas_call x1, Pallas kernels, attention(): pl.pallas_call(functools.partial(attention_body, rows, tiles, len(joined_...  25.6 us
    all_gather x1, waiting for transfers between devices, ring_gather(): lax.all_gather(own, 'batch', axis=0, tiled=True, axis_index_groups=[ring_...  17.5 us
    pallas_call x1, Pallas kernels, spread(): pl.pallas_call(spread_body, grid=(steps,), in_specs=[pl.BlockSpec((n // s...  14.5 us
    pallas_call x1, Pallas kernels, mlp_weights(): pl.pallas_call(functools.partial(mlp_weights_body, down), grid=(down + ha...  12.3 us
    unnamed x48, local copies, waits for them, and re-layouts  10.6 us
    pallas_call x1, Pallas kernels, grad_in_terms(): pl.pallas_call(functools.partial(grad_in_body, len(grad_joined)), grid_sp...  9.72 us
    reduce_scatter x1, waiting for transfers between devices, ring_scatter(): lax.psum_scatter(values, 'batch', scatter_dimension=0, tiled=True, axis_i...  9.08 us
  transfers between devices with their start and end apart: 15, of which 9 were waited for; matrix products, arithmetic and copies ran while one was open for 12% of the time, Pallas kernels for 26%

commit v1 on v0

--- a/solution.py
+++ b/solution.py
@@ -295,7 +295,8 @@
     width = whole.shape[1]
     mlp_rows, heads_rows = 2 * units // n, 2 * width // n
     assert whole.shape[0] == n * (mlp_rows + heads_rows) and mlp_rows % heads_rows == 0
-    steps = width // 128
+    lines = 256
+    steps = width // lines
     block = 2 * units // steps
     inner = 2 * width - columns
     across = width // block
@@ -318,8 +319,8 @@
         out_specs=[
             pl.BlockSpec((block, width), lambda i: (jnp.minimum(i, steps // 2 - 1), 0)),
             pl.BlockSpec((block, width), lambda i: (later(i) % across, later(i) // across)),
-            pl.BlockSpec((128, columns), lambda i: (i, 0)),
-            pl.BlockSpec((inner, 128), lambda i: (0, i)),
+            pl.BlockSpec((lines, columns), lambda i: (i, 0)),
+            pl.BlockSpec((inner, lines), lambda i: (0, i)),
         ],
         out_shape=[
             jax.ShapeDtypeStruct((units, width), WIDE),

time: 262 us -> 260 us (level)
  transfers between devices with their start and end apart: 15 -> 15, of which waited for: 9 -> 9; matrix products, arithmetic and copies ran while one was open for 12% -> 12% of each run, Pallas kernels for 26% -> 27%
where the time goes in v1:
time: 260 us; the launch traced here: 259 us
  Pallas kernels  101 us (39%)
  waiting for transfers between devices  89.2 us (34%)
  local copies, waits for them, and re-layouts  22.5 us (9%)
  between operations  14.1 us (5%)
  other arithmetic  14 us (5%)
  starting transfers between devices  12.5 us (5%)
  matrix products  6.4 us (2%)
    ppermute x5, waiting for transfers between devices, swap(): return lax.ppermute(values, axis, [(0, 1), (1, 0)])  57 us
    pallas_call x1, Pallas kernels, attention(): pl.pallas_call(functools.partial(attention_body, rows, tiles, len(joined_...  25.6 us
    all_gather x1, waiting for transfers between devices, ring_gather(): lax.all_gather(own, 'batch', axis=0, tiled=True, axis_index_groups=[ring_...  17.5 us
    pallas_call x1, Pallas kernels, spread(): pl.pallas_call(spread_body, grid=(steps,), in_specs=[pl.BlockSpec((n // s...  12.7 us
    pallas_call x1, Pallas kernels, mlp_weights(): pl.pallas_call(functools.partial(mlp_weights_body, down), grid=(down + ha...  12.3 us
    unnamed x48, local copies, waits for them, and re-layouts  10.6 us
    pallas_call x1, Pallas kernels, grad_in_terms(): pl.pallas_call(functools.partial(grad_in_body, len(grad_joined)), grid_sp...  9.72 us
    reduce_scatter x1, waiting for transfers between devices, ring_scatter(): lax.psum_scatter(values, 'batch', scatter_dimension=0, tiled=True, axis_i...  9.08 us
  transfers between devices with their start and end apart: 15, of which 9 were waited for; matrix products, arithmetic and copies ran while one was open for 12% of the time, Pallas kernels for 27%

profile of v1, /device:TPU:0, one launch (start us, length us, event | category | flops | bytes accessed | tf_op | source)
XLA Modules:
  0.0 259.4 jit_solution(5993778636202049818)
XLA Ops:
  7.2 3.0 %collective-permute-start = (bf16[896,512]{1,0:T(8,128)(2,1)}, bf16[896,512]{1,0:T(8,128)(2,1)S(1)}, u32[]{:S(2)}, u32[]{:S(2)}) collective-permute-start(bf16[896,512]{1,0:T(8,128)(2,1)} %tokens_ref.3), channel_id=1, source_target_pairs={{0,1},{1,0},{2,3},{3,2},{4,5},{5,4},{6,7},{7,6},{8,9},{9,8},{10,11... | collective-permute-start | bytes 2752520 | tf_op jit(solution)/shard_map/ppermute | solution.py:26
  10.2 0.1 collective-permute-start.1
  10.3 0.8 reshape.151
  11.1 1.4 fusion.3
  12.5 1.4 convert_reduce_fusion
  13.8 0.7 broadcast_compare_fusion
  14.5 3.3 %select_select_fusion = s32[896]{0:T(1024)S(1)} fusion(pred[896]{0:T(1024)(128)(4,1)} %constant.158, pred[896]{0:T(1024)(128)(4,1)} %constant.159, pred[896]{0:T(1024)(128)(4,1)} %constant.160, s32[]{:T(128)} %bitcast.4, s32[]{:T(128)} %bitcast.1, s32[]{:T(128)} %bitcast.2, s32[]{:T(128)} %bitcast.3), kind=kLoop, calls=%fused_computation.17 | loop fusion | flops 2688 | bytes 6288 | tf_op jit(solution)/shard_map/jit(_take)/gather | solution.py:795
  17.8 0.1 select_convert_fusion
  17.9 13.7 %collective-permute-done.other_ref = bf16[896,512]{1,0:T(8,128)(2,1)S(1)} collective-permute-done((bf16[896,512]{1,0:T(8,128)(2,1)}, bf16[896,512]{1,0:T(8,128)(2,1)S(1)}, u32[]{:S(2)}, u32[]{:S(2)}) %collective-permute-start) | collective-permute-done | bytes 917536 | tf_op jit(solution)/shard_map/ppermute | solution.py:26
  31.6 0.9 copy-done.19
  32.6 4.6 %input_norm.1 = (bf16[896,1024]{1,0:T(8,128)(2,1)}, f32[896,128]{1,0:T(8,128)}) custom-call(s32[1]{0:T(128)} %bitcast.side_ref, bf16[896,512]{1,0:T(8,128)(2,1)} %tokens_ref.3, bf16[896,512]{1,0:T(8,128)(2,1)} %copy-done.19, f32[1,1024]{1,0:T(1,128)} %bitcast.34), custom_call_target="tpu_custom_call" | custom-call | flops 1024 | bytes 1024 | tf_op jit(solution)/shard_map/input_norm/pallas_call | solution.py:102
  37.1 1.5 copy-done.1
  38.6 8.8 %mlp_forward.1 = (bf16[896,2048]{1,0:T(8,128)(2,1)S(1)}, bf16[896,2048]{1,0:T(8,128)(2,1)S(1)}) custom-call(bf16[896,1024]{1,0:T(8,128)(2,1)S(1)} %copy-done.1, bf16[1024,2048]{1,0:T(8,128)(2,1)} %w_up_ref, f32[1,2048]{1,0:T(1,128)S(1)} %bitcast.27), custom_call_target="tpu_custom_call" | custom-call | flops 1024 | bytes 1024 | tf_op jit(solution)/shard_map/mlp_forward/pallas_call | solution.py:53
  47.4 3.1 %collective-permute-done.1.other_ref = bf16[896,512]{1,0:T(8,128)(2,1)S(1)} collective-permute-done((bf16[896,512]{1,0:T(8,128)(2,1)}, bf16[896,512]{1,0:T(8,128)(2,1)S(1)}, u32[]{:S(2)}, u32[]{:S(2)}) %collective-permute-start.1) | collective-permute-done | bytes 917536 | tf_op jit(solution)/shard_map/ppermute | solution.py:26
  50.5 6.9 %mlp_slope.1 = (bf16[896,2048]{1,0:T(8,128)(2,1)S(1)}, f32[1,2048]{1,0:T(1,128)S(1)}, bf16[896,1024]{1,0:T(8,128)(2,1)S(1)}) custom-call(s32[1]{0:T(128)} %bitcast.side_ref, bf16[896,512]{1,0:T(8,128)(2,1)S(1)} %copy-done.9, bf16[896,512]{1,0:T(8,128)(2,1)S(1)} %collective-permute-done.1.other_ref, bf16[2048,1024]{1,0:T(8,128)(2,1)} %w_down_ref, ...), custom_call_target="tpu_custom_call" | custom-call | flops 1024 | bytes 1024 | tf_op jit(solution)/shard_map/mlp_slope/pallas_call | solution.py:152
  57.4 12.3 %mlp_weights.1 = bf16[4096,1024]{1,0:T(8,128)(2,1)} custom-call(bf16[896,2048]{1,0:T(8,128)(2,1)S(1)} %get-tuple-element.105.hidden_ref, bf16[896,1024]{1,0:T(8,128)(2,1)S(1)} %get-tuple-element.87.piece_ref, bf16[896,1024]{1,0:T(8,128)(2,1)S(1)} %copy-done.2, bf16[896,2048]{1,0:T(8,128)(2,1)S(1)} %get-tuple-element.99.grad_pre_ref), custom_call_target="tpu_custom_call" | custom-call | flops 1024 | bytes 1024 | tf_op jit(solution)/shard_map/mlp_weights/pallas_call | solution.py:213
  69.7 1.8 copy-done.5
  71.5 1.2 copy-done.10
  72.8 0.1 copy.43.refs_2_
  72.9 1.0 copy-done.15
  74.0 2.9 %fusion.refs_1_ = bf16[512,896]{1,0:T(8,128)(2,1)S(1)} fusion(bf16[896,1024]{1,0:T(8,128)(2,1)} %copy-done.10, bf16[512,1024]{1,0:T(8,128)(2,1)S(1)} %copy-done.15), kind=kOutput, calls=%fused_computation.5 | convolution fusion | flops 939982848 | bytes 3801088 | tf_op jit(solution)/shard_map/dot_general | solution.py:20
  76.9 3.5 %convolution_bitcast_fusion.refs_0_ = f32[1536,896]{1,0:T(8,128)S(1)} fusion(bf16[896,1024]{1,0:T(8,128)(2,1)S(1)} %copy-done.2, bf16[1024,1536]{1,0:T(8,128)(2,1)S(1)} %copy-done.18), kind=kOutput, calls=%fused_computation.1 | convolution fusion | flops 2818572288 | bytes 10485760 | tf_op jit(solution)/shard_map/dot_general | solution.py:20
  80.4 25.6 %attention_both.1 = (bf16[512,896]{1,0:T(8,128)(2,1)S(1)}, bf16[896,1536]{1,0:T(8,128)(2,1)S(1)}, f32[128,128]{1,0:T(8,128)S(1)}) custom-call(f32[1536,896]{1,0:T(8,128)S(1)} %convolution_bitcast_fusion.refs_0_, bf16[512,896]{1,0:T(8,128)(2,1)S(1)} %fusion.refs_1_, f32[128,1]{1,0:T(8,128)S(1)} %copy.43.refs_2_, ...), custom_call_target="tpu_custom_call" | custom-call | flops 1024 | bytes 1024 | tf_op jit(solution)/shard_map/attention_both/pallas_call | solution.py:638
  106.1 6.2 %heads_weights.1 = bf16[2048,1024]{1,0:T(8,128)(2,1)} custom-call(bf16[896,1024]{1,0:T(8,128)(2,1)S(1)} %copy-done.2, bf16[896,1024]{1,0:T(8,128)(2,1)S(1)} %copy-done.11, bf16[896,1536]{1,0:T(8,128)(2,1)S(1)} %get-tuple-element.101.grad_joined_ref.refs_0_, bf16[512,896]{1,0:T(8,128)(2,1)S(1)} %get-tuple-element.107.attended_ref.refs_0_), custom_call_target="tpu_custom_call" | custom-call | flops 1024 | bytes 1024 | tf_op jit(solution)/shard_map/heads_weights/pallas_call | solution.py:257
  112.3 1.9 constant_dynamic-slice_fusion
  114.2 0.1 collective-permute-start.2
  114.3 4.3 %collective-permute-done.2 = bf16[2,2,2,1,128,1024]{5,4,3,2,1,0:T(8,128)(2,1)} collective-permute-done((bf16[2,2,2,1,128,1024]{5,4,3,2,1,0:T(8,128)(2,1)S(1)}, bf16[2,2,2,1,128,1024]{5,4,3,2,1,0:T(8,128)(2,1)}, u32[]{:S(2)}, u32[]{:S(2)}) %collective-permute-start.2) | collective-permute-done | bytes 2097184 | tf_op jit(solution)/shard_map/ppermute | solution.py:695
  118.6 4.9 %add_convert_fusion = bf16[2,2,2,1,128,1024]{5,4,3,2,1,0:T(8,128)(2,1)} fusion(bf16[2,2,2,1,128,1024]{5,4,3,2,1,0:T(8,128)(2,1)} %collective-permute-done.2, bf16[2,2,2,2,128,1024]{5,4,3,2,1,0:T(8,128)(2,1)} %bitcast.32, s32[]{:T(128)S(6)} %select_n.57), kind=kLoop, calls=%fused_computation | loop fusion | flops 4194304 | bytes 6291460 | tf_op jit(solution)/shard_map/convert_element_type | solution.py:703
  123.4 9.1 %reduce-scatter.3.cloned.1.call-done = bf16[256,1024]{1,0:T(8,128)(2,1)} async-done(((bf16[4096,1024]{1,0:T(8,128)(2,1)}), bf16[256,1024]{1,0:T(8,128)(2,1)}) %reduce-scatter.3.cloned.1.call-update) | async-done | bytes 524304 | tf_op jit(solution)/shard_map/reduce_scatter | solution.py:677
  132.6 2.0 copy-done.6
  134.6 9.7 %grad_in_terms.1 = (bf16[896,512]{1,0:T(8,128)(2,1)S(1)}, f32[896,512]{1,0:T(8,128)S(1)}) custom-call(s32[1]{0:T(128)} %bitcast.side_ref, bf16[1024,1536]{1,0:T(8,128)(2,1)} %w_qkv_ref, bf16[896,2048]{1,0:T(8,128)(2,1)S(1)} %copy-done.6, bf16[1024,2048]{1,0:T(8,128)(2,1)} %w_up_ref, bf16[896,1536]{1,0:T(8,128)(2,1)S(1)} %copy-done.8), custom_call_target="tpu_custom_call" | custom-call | flops 1024 | bytes 1024 | tf_op jit(solution)/shard_map/grad_in_terms/pallas_call | solution.py:420
  144.4 1.2 copy-done.14
  145.6 0.9 collective-permute-start.3
  146.5 5.8 %output_terms.1 = (bf16[896,512]{1,0:T(8,128)(2,1)S(1)}, f32[896,512]{1,0:T(8,128)S(1)}) custom-call(s32[1]{0:T(128)} %bitcast.side_ref, bf16[512,1024]{1,0:T(8,128)(2,1)S(1)} %copy-done.16, bf16[896,2048]{1,0:T(8,128)(2,1)S(1)} %copy-done.4, bf16[2048,1024]{1,0:T(8,128)(2,1)S(1)} %copy-done, bf16[512,896]{1,0:T(8,128)(2,1)S(1)} %copy-done.13), custom_call_target="tpu_custom_call" | custom-call | flops 1024 | bytes 1024 | tf_op jit(solution)/shard_map/output_terms/pallas_call | solution.py:365
  152.3 1.0 dynamic_update_slice.6
  153.2 14.9 %collective-permute-done.3.arrived_ref = bf16[896,512]{1,0:T(8,128)(2,1)} collective-permute-done((bf16[896,512]{1,0:T(8,128)(2,1)S(1)}, bf16[896,512]{1,0:T(8,128)(2,1)}, u32[]{:S(2)}, u32[]{:S(2)}) %collective-permute-start.3) | collective-permute-done | bytes 917536 | tf_op jit(solution)/shard_map/ppermute | solution.py:26
  168.1 0.1 reduce-scatter.5.cloned.1.call-done
  168.2 1.7 constant_dynamic-update-slice_fusion
  169.9 0.1 reduce_sum.19
  170.0 0.1 reshape.156
  170.1 0.1 copy.44
  170.2 1.6 collective-permute-start.5
  171.8 3.6 %grad_in_hat.1 = (f32[896,512]{1,0:T(8,128)}, f32[896,128]{1,0:T(8,128)}, f32[1,512]{1,0:T(1,128)}) custom-call(s32[1]{0:T(128)} %bitcast.side_ref, f32[896,512]{1,0:T(8,128)} %copy-done.14, bf16[896,512]{1,0:T(8,128)(2,1)} %collective-permute-done.3.arrived_ref, bf16[896,512]{1,0:T(8,128)(2,1)} %tokens_ref.3, f32[896,128]{1,0:T(8,128)} %get-tuple-element.109.stats_ref, ...), custom_call_target="tpu_custom_call" | custom-call | flops 1024 | bytes 1024 | tf_op jit(solution)/shard_map/grad_in_hat/pallas_call | solution.py:471
  175.4 1.1 slice_bitcast_fusion.1
  176.6 0.5 collective-permute-start.4
  177.0 25.3 %collective-permute-done.4 = f32[2,960]{0,1:T(8,128)S(1)} collective-permute-done((f32[2,960]{0,1:T(8,128)S(1)}, f32[2,960]{0,1:T(8,128)S(1)}, u32[]{:S(2)}, u32[]{:S(2)}) %collective-permute-start.4) | collective-permute-done | bytes 7712 | tf_op jit(solution)/shard_map/ppermute | solution.py:26
  202.3 0.8 copy-done.21
  203.1 0.1 copy.46
  203.2 0.1 reshape.157
  203.3 0.7 pad_maximum_fusion.1
  204.0 0.7 collective-permute-start.7
  204.7 1.1 collective-permute-start.6
  205.8 1.8 slice_bitcast_fusion.other_ref
  207.7 4.7 %grad_in_finish.1 = bf16[896,512]{1,0:T(8,128)(2,1)} custom-call(bf16[896,512]{1,0:T(8,128)(2,1)} %cotangent_ref.1, bf16[896,512]{1,0:T(8,128)(2,1)} %tokens_ref.3, f32[896,128]{1,0:T(8,128)} %get-tuple-element.109.stats_ref, f32[896,512]{1,0:T(8,128)} %get-tuple-element.117.hat_ref, f32[896,128]{1,0:T(8,128)} %get-tuple-element.118.sums_ref, ...), custom_call_target="tpu_custom_call" | custom-call | flops 1024 | bytes 1024 | tf_op jit(solution)/shard_map/grad_in_finish/pallas_call | solution.py:508
  212.4 3.4 %collective-permute-start.11 = (f32[3200]{0:T(1024)S(1)}, f32[3200]{0:T(1024)S(1)}, u32[]{:S(2)}, u32[]{:S(2)}) collective-permute-start(f32[3200]{0:T(1024)S(1)} %add_add_fusion.1), channel_id=1, source_target_pairs={{0,24},{2,26},{4,28},{6,30},{8,16},{10,18},{12,20},{14,22},{16,8},... | collective-permute-start | bytes 38408 | tf_op jit(solution)/shard_map/ppermute | solution.py:695
  215.8 0.4 collective-permute-start.10
  216.2 0.6 collective-permute-start.9
  216.8 2.8 %add_convert_fusion.1 = bf16[896,512]{1,0:T(8,128)(2,1)} fusion(f32[896,512]{1,0:T(8,128)S(1)} %get-tuple-element.108, bf16[896,512]{1,0:T(8,128)(2,1)} %collective-permute-done.5, bf16[896,512]{1,0:T(8,128)(2,1)} %tokens_ref.3, f32[512]{0:T(512)S(1)} %copy-done.23), kind=kLoop, calls=%fused_computation.2 | loop fusion | flops 2752512 | bytes 4589568 | tf_op jit(solution)/shard_map/convert_element_type | solution.py:863
  219.7 1.1 collective-permute-done.10
  220.8 0.6 slice.62
  221.4 0.6 slice.52
  222.1 0.6 fusion.2
  222.7 17.5 %all-gather.2.cloned.1.call-done = bf16[6144,1024]{1,0:T(8,128)(2,1)} async-done(((bf16[384,1024]{1,0:T(8,128)(2,1)}), bf16[6144,1024]{1,0:T(8,128)(2,1)}) %all-gather.2.cloned.1.call-update) | async-done | bytes 12582928 | tf_op jit(solution)/shard_map/all_gather | solution.py:691
  240.2 12.7 %spread.1 = (f32[2048,1024]{1,0:T(8,128)}, f32[1024,2048]{1,0:T(8,128)}, f32[1024,1536]{1,0:T(8,128)}, f32[512,1024]{1,0:T(8,128)}) custom-call(bf16[16,384,1024]{2,1,0:T(8,128)(2,1)} %bitcast.28, bf16[16,3,128,1024]{3,2,1,0:T(8,128)(2,1)} %bitcast.29, bf16[16,3,128,1024]{3,2,1,0:T(8,128)(2,1)} %bitcast.30), custom_call_target="tpu_custom_call" | custom-call | flops 1024 | bytes 1024 | tf_op jit(solution)/shard_map/spread/pallas_call | solution.py:311
  (59 shorter events, 0.3 us)
Async XLA Ops:
  7.2 29.9 %copy-start.17 = (f32[2048]{0:T(1024)S(1)}, f32[2048]{0:T(1024)}, u32[]{:S(2)}) copy-start(f32[2048]{0:T(1024)} %param.20) | copy-start | bytes 24580
  7.2 125.3 %reduce-scatter.3.cloned.1.call-start = ((), (), s32[]{:S(2)}) async-start(), calls=%async_computation.2 | async-start | bytes 8912896 | tf_op jit(solution)/shard_map/reduce_scatter | solution.py:677
  7.2 24.4 %collective-permute-start = (bf16[896,512]{1,0:T(8,128)(2,1)}, bf16[896,512]{1,0:T(8,128)(2,1)S(1)}, u32[]{:S(2)}, u32[]{:S(2)}) collective-permute-start(bf16[896,512]{1,0:T(8,128)(2,1)} %tokens_ref.3), channel_id=1, source_target_pairs={{0,1},{1,0},{2,3},{3,2},{4,5},{5,4},{6,7},{7,6},{8,9},{9,8},{10,11... | collective-permute-start | bytes 2752520 | tf_op jit(solution)/shard_map/ppermute | solution.py:26
  10.2 40.2 %collective-permute-start.1 = (bf16[896,512]{1,0:T(8,128)(2,1)}, bf16[896,512]{1,0:T(8,128)(2,1)S(1)}, u32[]{:S(2)}, u32[]{:S(2)}) collective-permute-start(bf16[896,512]{1,0:T(8,128)(2,1)} %cotangent_ref.1), channel_id=1, source_target_pairs={{0,1},{1,0},{2,3},{3,2},{4,5},{5,4},{6,7},{7,6},{8,9},{9,8},{10,11... | collective-permute-start | bytes 2752520 | tf_op jit(solution)/shard_map/ppermute | solution.py:26
  31.6 0.9 copy-start.19
  37.1 1.5 copy-start.1
  38.6 11.8 %copy-start.9 = (bf16[896,512]{1,0:T(8,128)(2,1)S(1)}, bf16[896,512]{1,0:T(8,128)(2,1)}, u32[]{:S(2)}) copy-start(bf16[896,512]{1,0:T(8,128)(2,1)} %cotangent_ref.1) | copy-start | bytes 2752516
  47.4 10.0 %copy-start.3 = (bf16[896,2048]{1,0:T(8,128)(2,1)}, bf16[896,2048]{1,0:T(8,128)(2,1)S(1)}, u32[]{:S(2)}) copy-start(bf16[896,2048]{1,0:T(8,128)(2,1)S(1)} %get-tuple-element.105.hidden_ref) | copy-start | bytes 11010052
  50.5 6.9 %copy-start.2 = (bf16[896,1024]{1,0:T(8,128)(2,1)S(1)}, bf16[896,1024]{1,0:T(8,128)(2,1)}, u32[]{:S(2)}) copy-start(bf16[896,1024]{1,0:T(8,128)(2,1)} %get-tuple-element.86.normed_ref) | copy-start | bytes 5505028
  69.7 1.8 copy-start.5
  71.5 1.2 copy-start.10
  72.7 1.2 copy-start.15
  72.7 95.5 %reduce-scatter.5.cloned.1.call-start = ((), (), s32[]{:S(2)}) async-start(), calls=%async_computation.3 | async-start | bytes 2359296 | tf_op jit(solution)/shard_map/reduce_scatter | solution.py:685
  73.9 2.9 %copy-start.18 = (bf16[1024,1536]{1,0:T(8,128)(2,1)S(1)}, bf16[1024,1536]{1,0:T(8,128)(2,1)}, u32[]{:S(2)}) copy-start(bf16[1024,1536]{1,0:T(8,128)(2,1)} %w_qkv_ref) | copy-start | bytes 9437188
  80.4 25.7 %copy-start.11 = (bf16[896,1024]{1,0:T(8,128)(2,1)S(1)}, bf16[896,1024]{1,0:T(8,128)(2,1)}, u32[]{:S(2)}) copy-start(bf16[896,1024]{1,0:T(8,128)(2,1)} %copy-done.10) | copy-start | bytes 5505028
  106.0 6.2 %copy-start.7 = (bf16[896,1536]{1,0:T(8,128)(2,1)}, bf16[896,1536]{1,0:T(8,128)(2,1)S(1)}, u32[]{:S(2)}) copy-start(bf16[896,1536]{1,0:T(8,128)(2,1)S(1)} %get-tuple-element.101.grad_joined_ref.refs_0_) | copy-start | bytes 8257540
  106.0 6.2 %copy-start.12 = (bf16[512,896]{1,0:T(8,128)(2,1)}, bf16[512,896]{1,0:T(8,128)(2,1)S(1)}, u32[]{:S(2)}) copy-start(bf16[512,896]{1,0:T(8,128)(2,1)S(1)} %get-tuple-element.107.attended_ref.refs_0_) | copy-start | bytes 2752516
  114.2 4.4 %collective-permute-start.2 = (bf16[2,2,2,1,128,1024]{5,4,3,2,1,0:T(8,128)(2,1)S(1)}, bf16[2,2,2,1,128,1024]{5,4,3,2,1,0:T(8,128)(2,1)}, u32[]{:S(2)}, u32[]{:S(2)}) collective-permute-start(bf16[2,2,2,1,128,1024]{5,4,3,2,1,0:T(8,128)(2,1)S(1)} %constant_dynamic-slice_fusion), channel_id=1, source_target_pairs={{0,2},{2,0},{4,6},{6,4},{8,10},{10,8},{12,14},{14,12},{16,18},{18,... | collective-permute-start | bytes 6291464 | tf_op jit(solution)/shard_map/ppermute | solution.py:695
  118.6 14.0 %copy-start.8 = (bf16[896,1536]{1,0:T(8,128)(2,1)S(1)}, bf16[896,1536]{1,0:T(8,128)(2,1)}, u32[]{:S(2)}) copy-start(bf16[896,1536]{1,0:T(8,128)(2,1)} %copy-done.7) | copy-start | bytes 8257540
  132.5 107.7 %all-gather.2.cloned.1.call-start = ((), (), s32[]{:S(2)}) async-start(), calls=%async_computation.4 | async-start | bytes 13369344 | tf_op jit(solution)/shard_map/all_gather | solution.py:691
  132.6 2.0 copy-start.6
  134.6 11.8 %copy-start = (bf16[2048,1024]{1,0:T(8,128)(2,1)S(1)}, bf16[2048,1024]{1,0:T(8,128)(2,1)}, u32[]{:S(2)}) copy-start(bf16[2048,1024]{1,0:T(8,128)(2,1)} %w_down_ref) | copy-start | bytes 12582916
  134.6 11.8 %copy-start.4 = (bf16[896,2048]{1,0:T(8,128)(2,1)S(1)}, bf16[896,2048]{1,0:T(8,128)(2,1)}, u32[]{:S(2)}) copy-start(bf16[896,2048]{1,0:T(8,128)(2,1)} %copy-done.3) | copy-start | bytes 11010052
  134.6 11.8 %copy-start.13 = (bf16[512,896]{1,0:T(8,128)(2,1)S(1)}, bf16[512,896]{1,0:T(8,128)(2,1)}, u32[]{:S(2)}) copy-start(bf16[512,896]{1,0:T(8,128)(2,1)} %copy-done.12) | copy-start | bytes 2752516
  134.6 11.8 %copy-start.16 = (bf16[512,1024]{1,0:T(8,128)(2,1)S(1)}, bf16[512,1024]{1,0:T(8,128)(2,1)}, u32[]{:S(2)}) copy-start(bf16[512,1024]{1,0:T(8,128)(2,1)} %w_out_ref) | copy-start | bytes 3145732
  144.3 1.2 copy-start.14
  145.6 6.7 %copy-start.20 = (bf16[256,1024]{1,0:T(8,128)(2,1)S(1)}, bf16[256,1024]{1,0:T(8,128)(2,1)}, u32[]{:S(2)}) copy-start(bf16[256,1024]{1,0:T(8,128)(2,1)} %reduce-scatter.3.cloned.1.call-done) | copy-start | bytes 1572868
  145.6 22.6 %collective-permute-start.3 = (bf16[896,512]{1,0:T(8,128)(2,1)S(1)}, bf16[896,512]{1,0:T(8,128)(2,1)}, u32[]{:S(2)}, u32[]{:S(2)}) collective-permute-start(bf16[896,512]{1,0:T(8,128)(2,1)S(1)} %get-tuple-element.102), channel_id=1, source_target_pairs={{0,1},{1,0},{2,3},{3,2},{4,5},{5,4},{6,7},{7,6},{8,9},{9,8},{10,11... | collective-permute-start | bytes 2752520 | tf_op jit(solution)/shard_map/ppermute | solution.py:26
  170.2 42.1 %collective-permute-start.5 = (bf16[896,512]{1,0:T(8,128)(2,1)S(1)}, bf16[896,512]{1,0:T(8,128)(2,1)}, u32[]{:S(2)}, u32[]{:S(2)}) collective-permute-start(bf16[896,512]{1,0:T(8,128)(2,1)S(1)} %get-tuple-element.111), channel_id=1, source_target_pairs={{0,1},{1,0},{2,3},{3,2},{4,5},{5,4},{6,7},{7,6},{8,9},{9,8},{10,11... | collective-permute-start | bytes 2752520 | tf_op jit(solution)/shard_map/ppermute | solution.py:26
  176.6 25.8 %collective-permute-start.4 = (f32[2,960]{0,1:T(8,128)S(1)}, f32[2,960]{0,1:T(8,128)S(1)}, u32[]{:S(2)}, u32[]{:S(2)}) collective-permute-start(f32[2,960]{0,1:T(8,128)S(1)} %pad_maximum_fusion), channel_id=1, source_target_pairs={{0,1},{1,0},{2,3},{3,2},{4,5},{5,4},{6,7},{7,6},{8,9},{9,8},{10,11... | collective-permute-start | bytes 23048 | tf_op jit(solution)/shard_map/ppermute | solution.py:26
  202.3 0.8 copy-start.21
  204.0 8.3 %collective-permute-start.8 = (f32[3200]{0:T(1024)S(1)}, f32[3200]{0:T(1024)S(1)}, u32[]{:S(2)}, u32[]{:S(2)}) collective-permute-start(f32[3200]{0:T(1024)S(1)} %pad_maximum_fusion.1), channel_id=1, source_target_pairs={{0,6},{2,4},{4,2},{6,0},{8,14},{10,12},{12,10},{14,8},{16,22},{18,... | collective-permute-start | bytes 38408 | tf_op jit(solution)/shard_map/ppermute | solution.py:695
  204.0 8.3 %collective-permute-start.7 = (f32[3200]{0:T(1024)S(1)}, f32[3200]{0:T(1024)S(1)}, u32[]{:S(2)}, u32[]{:S(2)}) collective-permute-start(f32[3200]{0:T(1024)S(1)} %pad_maximum_fusion.1), channel_id=1, source_target_pairs={{0,4},{2,6},{4,0},{6,2},{8,12},{10,14},{12,8},{14,10},{16,20},{18,... | collective-permute-start | bytes 38408 | tf_op jit(solution)/shard_map/ppermute | solution.py:695
  204.7 7.6 %collective-permute-start.6 = (f32[3200]{0:T(1024)S(1)}, f32[3200]{0:T(1024)S(1)}, u32[]{:S(2)}, u32[]{:S(2)}) collective-permute-start(f32[3200]{0:T(1024)S(1)} %pad_maximum_fusion.1), channel_id=1, source_target_pairs={{0,2},{2,0},{4,6},{6,4},{8,10},{10,8},{12,14},{14,12},{16,18},{18,... | collective-permute-start | bytes 38408 | tf_op jit(solution)/shard_map/ppermute | solution.py:695
  207.7 4.7 %copy-start.22 = (f32[1,512]{1,0:T(1,128)S(1)}, f32[1,512]{1,0:T(1,128)}, u32[]{:S(2)}) copy-start(f32[1,512]{1,0:T(1,128)} %get-tuple-element.122) | copy-start | bytes 6148
  207.7 9.2 %copy-start.23 = (f32[512]{0:T(512)S(1)}, f32[512]{0:T(512)}, u32[]{:S(2)}) copy-start(f32[512]{0:T(512)} %param.22) | copy-start | bytes 6148
  212.4 7.3 %collective-permute-start.11 = (f32[3200]{0:T(1024)S(1)}, f32[3200]{0:T(1024)S(1)}, u32[]{:S(2)}, u32[]{:S(2)}) collective-permute-start(f32[3200]{0:T(1024)S(1)} %add_add_fusion.1), channel_id=1, source_target_pairs={{0,24},{2,26},{4,28},{6,30},{8,16},{10,18},{12,20},{14,22},{16,8},... | collective-permute-start | bytes 38408 | tf_op jit(solution)/shard_map/ppermute | solution.py:695
  215.8 5.1 %collective-permute-start.10 = (f32[3200]{0:T(1024)S(1)}, f32[3200]{0:T(1024)S(1)}, u32[]{:S(2)}, u32[]{:S(2)}) collective-permute-start(f32[3200]{0:T(1024)S(1)} %add_add_fusion.1), channel_id=1, source_target_pairs={{0,16},{2,18},{4,20},{6,22},{8,24},{10,26},{12,28},{14,30},{16,0},... | collective-permute-start | bytes 38408 | tf_op jit(solution)/shard_map/ppermute | solution.py:695
  216.2 4.6 %collective-permute-start.9 = (f32[3200]{0:T(1024)S(1)}, f32[3200]{0:T(1024)S(1)}, u32[]{:S(2)}, u32[]{:S(2)}) collective-permute-start(f32[3200]{0:T(1024)S(1)} %add_add_fusion.1), channel_id=1, source_target_pairs={{0,8},{2,10},{4,12},{6,14},{8,0},{10,2},{12,4},{14,6},{16,24},{18,... | collective-permute-start | bytes 38408 | tf_op jit(solution)/shard_map/ppermute | solution.py:695
Sparse Core Ops, SparseCore 0:
  72.9 59.5 reduce-scatter.2
  135.4 32.8 reduce-scatter.4
  170.4 69.7 all-gather.1

commit v2 on v1

--- a/solution.py
+++ b/solution.py
@@ -123,8 +123,10 @@
     )(side, mine, other, gain.reshape(1, 2 * half))
 
 
-def slope_body(side_ref, mine_ref, other_ref, w_ref, slope_ref, grad_pre_ref, bias_ref, piece_ref):
+def slope_body(side_ref, mine_ref, other_ref, w_ref, slope_ref, grad_pre_ref, bias_ref, piece_ref,
+               later_grad_ref, later_piece_ref):
     half = mine_ref.shape[1]
+    lines = later_piece_ref.shape[0]
 
     @pl.when(pl.program_id(0) == 0)
     def _():
@@ -138,13 +140,17 @@
     )
     low = (back * slope_ref[...].astype(WIDE)).astype(LOW)
     grad_pre_ref[...] = low
+    later_grad_ref[...] = low
     bias_ref[...] = jnp.sum(low.astype(WIDE), axis=0, keepdims=True)
+    start = pl.multiple_of(pl.program_id(0) * lines, lines)
+    later_piece_ref[...] = piece_ref[pl.ds(start, lines), :]
 
 
 def mlp_slope(side, mine, other, w_down, slope):
     rows, half = mine.shape
     units, width = w_down.shape
     block = 512
+    lines = rows * block // units
 
     def whole(i, s):
         return (0, 0)
@@ -164,12 +170,16 @@
                 pl.BlockSpec((rows, block), lambda i, s: (0, i)),
                 pl.BlockSpec((1, block), lambda i, s: (0, i)),
                 pl.BlockSpec((rows, width), whole),
+                pl.BlockSpec((rows, block), lambda i, s: (0, i)),
+                pl.BlockSpec((lines, width), lambda i, s: (i, 0)),
             ],
         ),
         out_shape=[
             jax.ShapeDtypeStruct((rows, units), LOW),
             jax.ShapeDtypeStruct((1, units), WIDE),
             jax.ShapeDtypeStruct((rows, width), LOW),
+            pltpu.HBM((rows, units), LOW),
+            pltpu.HBM((rows, width), LOW),
         ],
         compiler_params=pltpu.CompilerParams(vmem_limit_bytes=20 * MIB),
         cost_estimate=SHORT,
@@ -806,8 +816,10 @@
 
     normed, stats = input_norm(sides, tokens, other_tokens, ln_gain)
     hidden, slope = mlp_forward(normed, w_up, b_up)
-    grad_pre, grad_b_up, piece = mlp_slope(sides, cotangent, other_cotangent, w_down, slope)
-    mlp_part = mlp_weights(hidden, piece, normed, grad_pre)
+    grad_first, grad_b_up, piece_first, grad_pre, piece = mlp_slope(
+        sides, cotangent, other_cotangent, w_down, slope
+    )
+    mlp_part = mlp_weights(hidden, piece_first, normed, grad_first)
     mlp_own = ring_scatter(mlp_part, n_batch)
 
     def sent(part, bit):

time: 260 us -> 259 us (level)
  local copies, waits for them, and re-layouts: 22.5 us -> 18.3 us
    unnamed x48 -> x44, local copies, waits for them, and re-layouts: 10.6 us -> 6.32 us
where the time goes in v2:
time: 259 us; the launch traced here: 258 us
  Pallas kernels  102 us (39%)
  waiting for transfers between devices  89.4 us (35%)
  local copies, waits for them, and re-layouts  18.3 us (7%)
  between operations  14.1 us (5%)
  other arithmetic  14 us (5%)
  starting transfers between devices  13.2 us (5%)
  matrix products  6.51 us (3%)
    ppermute x5, waiting for transfers between devices, swap(): return lax.ppermute(values, axis, [(0, 1), (1, 0)])  56 us
    pallas_call x1, Pallas kernels, attention(): pl.pallas_call(functools.partial(attention_body, rows, tiles, len(joined_...  25.6 us
    all_gather x1, waiting for transfers between devices, ring_gather(): lax.all_gather(own, 'batch', axis=0, tiled=True, axis_index_groups=[ring_...  19 us
    pallas_call x1, Pallas kernels, spread(): pl.pallas_call(spread_body, grid=(steps,), in_specs=[pl.BlockSpec((n // s...  12.7 us
    pallas_call x1, Pallas kernels, mlp_weights(): pl.pallas_call(functools.partial(mlp_weights_body, down), grid=(down + ha...  12.3 us
    pallas_call x1, Pallas kernels, grad_in_terms(): pl.pallas_call(functools.partial(grad_in_body, len(grad_joined)), grid_sp...  9.72 us
    pallas_call x1, Pallas kernels, mlp_forward(): pl.pallas_call(mlp_body, grid=(units // block,), in_specs=[pl.BlockSpec((...  8.75 us
    pallas_call x1, Pallas kernels, mlp_slope(): pl.pallas_call(slope_body, grid_spec=pltpu.PrefetchScalarGridSpec(num_sca...  8.38 us
  transfers between devices with their start and end apart: 15, of which 9 were waited for; matrix products, arithmetic and copies ran while one was open for 12% of the time, Pallas kernels for 27%

profile of v2, /device:TPU:0, one launch (start us, length us, event | category | flops | bytes accessed | tf_op | source)
XLA Modules:
  0.0 257.7 jit_solution(17853434943109410531)
XLA Ops:
  7.2 0.0 reduce-scatter.3.cloned.1.call-start
  7.2 3.0 %collective-permute-start = (bf16[896,512]{1,0:T(8,128)(2,1)}, bf16[896,512]{1,0:T(8,128)(2,1)S(1)}, u32[]{:S(2)}, u32[]{:S(2)}) collective-permute-start(bf16[896,512]{1,0:T(8,128)(2,1)} %tokens_ref.3), channel_id=1, source_target_pairs={{0,1},{1,0},{2,3},{3,2},{4,5},{5,4},{6,7},{7,6},{8,9},{9,8},{10,11... | collective-permute-start | bytes 2752520 | tf_op jit(solution)/shard_map/ppermute | solution.py:26
  10.2 0.1 collective-permute-start.1
  10.3 0.8 reshape.151
  11.1 1.4 fusion.3
  12.5 1.4 convert_reduce_fusion
  13.8 0.7 broadcast_compare_fusion
  14.5 3.3 %select_select_fusion = s32[896]{0:T(1024)S(1)} fusion(pred[896]{0:T(1024)(128)(4,1)} %constant.158, pred[896]{0:T(1024)(128)(4,1)} %constant.159, pred[896]{0:T(1024)(128)(4,1)} %constant.160, s32[]{:T(128)} %bitcast.4, s32[]{:T(128)} %bitcast.1, s32[]{:T(128)} %bitcast.2, s32[]{:T(128)} %bitcast.3), kind=kLoop, calls=%fused_computation.17 | loop fusion | flops 2688 | bytes 6288 | tf_op jit(solution)/shard_map/jit(_take)/gather | solution.py:805
  17.8 0.1 select_convert_fusion
  17.9 13.7 %collective-permute-done.other_ref = bf16[896,512]{1,0:T(8,128)(2,1)S(1)} collective-permute-done((bf16[896,512]{1,0:T(8,128)(2,1)}, bf16[896,512]{1,0:T(8,128)(2,1)S(1)}, u32[]{:S(2)}, u32[]{:S(2)}) %collective-permute-start) | collective-permute-done | bytes 917536 | tf_op jit(solution)/shard_map/ppermute | solution.py:26
  31.6 0.9 copy-done.17
  32.6 4.6 %input_norm.1 = (bf16[896,1024]{1,0:T(8,128)(2,1)}, f32[896,128]{1,0:T(8,128)}) custom-call(s32[1]{0:T(128)} %bitcast.side_ref, bf16[896,512]{1,0:T(8,128)(2,1)} %tokens_ref.3, bf16[896,512]{1,0:T(8,128)(2,1)} %copy-done.17, f32[1,1024]{1,0:T(1,128)} %bitcast.34), custom_call_target="tpu_custom_call" | custom-call | flops 1024 | bytes 1024 | tf_op jit(solution)/shard_map/input_norm/pallas_call | solution.py:102
  37.1 1.5 copy-done.1
  38.6 8.8 %mlp_forward.1 = (bf16[896,2048]{1,0:T(8,128)(2,1)S(1)}, bf16[896,2048]{1,0:T(8,128)(2,1)S(1)}) custom-call(bf16[896,1024]{1,0:T(8,128)(2,1)S(1)} %copy-done.1, bf16[1024,2048]{1,0:T(8,128)(2,1)} %w_up_ref, f32[1,2048]{1,0:T(1,128)S(1)} %bitcast.27), custom_call_target="tpu_custom_call" | custom-call | flops 1024 | bytes 1024 | tf_op jit(solution)/shard_map/mlp_forward/pallas_call | solution.py:53
  47.4 3.1 %collective-permute-done.1.other_ref = bf16[896,512]{1,0:T(8,128)(2,1)S(1)} collective-permute-done((bf16[896,512]{1,0:T(8,128)(2,1)}, bf16[896,512]{1,0:T(8,128)(2,1)S(1)}, u32[]{:S(2)}, u32[]{:S(2)}) %collective-permute-start.1) | collective-permute-done | bytes 917536 | tf_op jit(solution)/shard_map/ppermute | solution.py:26
  50.5 8.4 %mlp_slope.1 = (bf16[896,2048]{1,0:T(8,128)(2,1)S(1)}, f32[1,2048]{1,0:T(1,128)S(1)}, bf16[896,1024]{1,0:T(8,128)(2,1)S(1)}, bf16[896,2048]{1,0:T(8,128)(2,1)}, bf16[896,1024]{1,0:T(8,128)(2,1)}) custom-call(s32[1]{0:T(128)} %bitcast.side_ref, bf16[896,512]{1,0:T(8,128)(2,1)S(1)} %copy-done.7, bf16[896,512]{1,0:T(8,128)(2,1)S(1)} %collective-permute-done.1.other_ref, ...), custom_call_target="tpu_custom_call" | custom-call | flops 1024 | bytes 1024 | tf_op jit(solution)/shard_map/mlp_slope/pallas_call | solution.py:158
  58.9 12.3 %mlp_weights.1 = bf16[4096,1024]{1,0:T(8,128)(2,1)} custom-call(bf16[896,2048]{1,0:T(8,128)(2,1)S(1)} %get-tuple-element.109.hidden_ref, bf16[896,1024]{1,0:T(8,128)(2,1)S(1)} %get-tuple-element.86.piece_ref, bf16[896,1024]{1,0:T(8,128)(2,1)S(1)} %copy-done.2, bf16[896,2048]{1,0:T(8,128)(2,1)S(1)} %get-tuple-element.87.grad_pre_ref), custom_call_target="tpu_custom_call" | custom-call | flops 1024 | bytes 1024 | tf_op jit(solution)/shard_map/mlp_weights/pallas_call | solution.py:223
  71.2 0.0 reduce-scatter.5.cloned.1.call-start
  71.3 0.1 copy.43.refs_2_
  71.4 1.0 copy-done.13
  72.4 2.9 %fusion.refs_1_ = bf16[512,896]{1,0:T(8,128)(2,1)S(1)} fusion(bf16[896,1024]{1,0:T(8,128)(2,1)} %get-tuple-element.90.piece_ref, bf16[512,1024]{1,0:T(8,128)(2,1)S(1)} %copy-done.13), kind=kOutput, calls=%fused_computation.5 | convolution fusion | flops 939982848 | bytes 3801088 | tf_op jit(solution)/shard_map/dot_general | solution.py:20
  75.3 3.6 %convolution_bitcast_fusion.refs_0_ = f32[1536,896]{1,0:T(8,128)S(1)} fusion(bf16[896,1024]{1,0:T(8,128)(2,1)S(1)} %copy-done.2, bf16[1024,1536]{1,0:T(8,128)(2,1)S(1)} %copy-done.16), kind=kOutput, calls=%fused_computation.1 | convolution fusion | flops 2818572288 | bytes 10485760 | tf_op jit(solution)/shard_map/dot_general | solution.py:20
  78.9 25.6 %attention_both.1 = (bf16[512,896]{1,0:T(8,128)(2,1)S(1)}, bf16[896,1536]{1,0:T(8,128)(2,1)S(1)}, f32[128,128]{1,0:T(8,128)S(1)}) custom-call(f32[1536,896]{1,0:T(8,128)S(1)} %convolution_bitcast_fusion.refs_0_, bf16[512,896]{1,0:T(8,128)(2,1)S(1)} %fusion.refs_1_, f32[128,1]{1,0:T(8,128)S(1)} %copy.43.refs_2_, ...), custom_call_target="tpu_custom_call" | custom-call | flops 1024 | bytes 1024 | tf_op jit(solution)/shard_map/attention_both/pallas_call | solution.py:648
  104.6 6.2 %heads_weights.1 = bf16[2048,1024]{1,0:T(8,128)(2,1)} custom-call(bf16[896,1024]{1,0:T(8,128)(2,1)S(1)} %copy-done.2, bf16[896,1024]{1,0:T(8,128)(2,1)S(1)} %copy-done.12, bf16[896,1536]{1,0:T(8,128)(2,1)S(1)} %get-tuple-element.105.grad_joined_ref.refs_0_, bf16[512,896]{1,0:T(8,128)(2,1)S(1)} %get-tuple-element.111.attended_ref.refs_0_), custom_call_target="tpu_custom_call" | custom-call | flops 1024 | bytes 1024 | tf_op jit(solution)/shard_map/heads_weights/pallas_call | solution.py:267
  110.8 1.9 constant_dynamic-slice_fusion
  112.7 0.1 collective-permute-start.2
  112.8 4.5 %collective-permute-done.2 = bf16[2,2,2,1,128,1024]{5,4,3,2,1,0:T(8,128)(2,1)} collective-permute-done((bf16[2,2,2,1,128,1024]{5,4,3,2,1,0:T(8,128)(2,1)S(1)}, bf16[2,2,2,1,128,1024]{5,4,3,2,1,0:T(8,128)(2,1)}, u32[]{:S(2)}, u32[]{:S(2)}) %collective-permute-start.2) | collective-permute-done | bytes 2097184 | tf_op jit(solution)/shard_map/ppermute | solution.py:705
  117.4 4.9 %add_convert_fusion = bf16[2,2,2,1,128,1024]{5,4,3,2,1,0:T(8,128)(2,1)} fusion(bf16[2,2,2,1,128,1024]{5,4,3,2,1,0:T(8,128)(2,1)} %collective-permute-done.2, bf16[2,2,2,2,128,1024]{5,4,3,2,1,0:T(8,128)(2,1)} %bitcast.32, s32[]{:T(128)S(6)} %select_n.57), kind=kLoop, calls=%fused_computation | loop fusion | flops 4194304 | bytes 6291460 | tf_op jit(solution)/shard_map/convert_element_type | solution.py:713
  122.2 8.1 %reduce-scatter.3.cloned.1.call-done = bf16[256,1024]{1,0:T(8,128)(2,1)} async-done(((bf16[4096,1024]{1,0:T(8,128)(2,1)}), bf16[256,1024]{1,0:T(8,128)(2,1)}) %reduce-scatter.3.cloned.1.call-update) | async-done | bytes 524304 | tf_op jit(solution)/shard_map/reduce_scatter | solution.py:687
  130.4 0.0 all-gather.2.cloned.1.call-start
  130.4 2.0 copy-done.10
  132.5 9.7 %grad_in_terms.1 = (bf16[896,512]{1,0:T(8,128)(2,1)S(1)}, f32[896,512]{1,0:T(8,128)S(1)}) custom-call(s32[1]{0:T(128)} %bitcast.side_ref, bf16[1024,1536]{1,0:T(8,128)(2,1)} %w_qkv_ref, bf16[896,2048]{1,0:T(8,128)(2,1)S(1)} %copy-done.10, bf16[1024,2048]{1,0:T(8,128)(2,1)} %w_up_ref, bf16[896,1536]{1,0:T(8,128)(2,1)S(1)} %copy-done.6), custom_call_target="tpu_custom_call" | custom-call | flops 1024 | bytes 1024 | tf_op jit(solution)/shard_map/grad_in_terms/pallas_call | solution.py:430
  142.2 1.6 collective-permute-start.3
  143.9 5.7 %output_terms.1 = (bf16[896,512]{1,0:T(8,128)(2,1)S(1)}, f32[896,512]{1,0:T(8,128)S(1)}) custom-call(s32[1]{0:T(128)} %bitcast.side_ref, bf16[512,1024]{1,0:T(8,128)(2,1)S(1)} %copy-done.14, bf16[896,2048]{1,0:T(8,128)(2,1)S(1)} %copy-done.4, bf16[2048,1024]{1,0:T(8,128)(2,1)S(1)} %copy-done, bf16[512,896]{1,0:T(8,128)(2,1)S(1)} %copy-done.9), custom_call_target="tpu_custom_call" | custom-call | flops 1024 | bytes 1024 | tf_op jit(solution)/shard_map/output_terms/pallas_call | solution.py:375
  149.6 1.0 dynamic_update_slice.6
  150.6 14.8 %collective-permute-done.3.arrived_ref = bf16[896,512]{1,0:T(8,128)(2,1)} collective-permute-done((bf16[896,512]{1,0:T(8,128)(2,1)S(1)}, bf16[896,512]{1,0:T(8,128)(2,1)}, u32[]{:S(2)}, u32[]{:S(2)}) %collective-permute-start.3) | collective-permute-done | bytes 917536 | tf_op jit(solution)/shard_map/ppermute | solution.py:26
  165.4 1.4 reduce-scatter.5.cloned.1.call-done
  166.8 1.7 constant_dynamic-update-slice_fusion
  168.5 0.1 reduce_sum.19
  168.6 0.1 reshape.156
  168.7 0.1 copy.44
  168.8 1.5 collective-permute-start.5
  170.3 3.6 %grad_in_hat.1 = (f32[896,512]{1,0:T(8,128)}, f32[896,128]{1,0:T(8,128)}, f32[1,512]{1,0:T(1,128)}) custom-call(s32[1]{0:T(128)} %bitcast.side_ref, f32[896,512]{1,0:T(8,128)} %copy-done.11, bf16[896,512]{1,0:T(8,128)(2,1)} %collective-permute-done.3.arrived_ref, bf16[896,512]{1,0:T(8,128)(2,1)} %tokens_ref.3, f32[896,128]{1,0:T(8,128)} %get-tuple-element.113.stats_ref, ...), custom_call_target="tpu_custom_call" | custom-call | flops 1024 | bytes 1024 | tf_op jit(solution)/shard_map/grad_in_hat/pallas_call | solution.py:481
  173.9 1.2 slice_bitcast_fusion.1
  175.1 0.5 collective-permute-start.4
  175.6 24.4 %collective-permute-done.4 = f32[2,960]{0,1:T(8,128)S(1)} collective-permute-done((f32[2,960]{0,1:T(8,128)S(1)}, f32[2,960]{0,1:T(8,128)S(1)}, u32[]{:S(2)}, u32[]{:S(2)}) %collective-permute-start.4) | collective-permute-done | bytes 7712 | tf_op jit(solution)/shard_map/ppermute | solution.py:26
  200.1 0.8 copy-done.19
  200.9 0.1 copy.46
  200.9 0.1 reshape.157
  201.0 0.7 pad_maximum_fusion.1
  201.7 0.4 collective-permute-start.7
  202.1 1.5 collective-permute-start.6
  203.6 1.8 slice_bitcast_fusion.other_ref
  205.4 4.7 %grad_in_finish.1 = bf16[896,512]{1,0:T(8,128)(2,1)} custom-call(bf16[896,512]{1,0:T(8,128)(2,1)} %cotangent_ref.1, bf16[896,512]{1,0:T(8,128)(2,1)} %tokens_ref.3, f32[896,128]{1,0:T(8,128)} %get-tuple-element.113.stats_ref, f32[896,512]{1,0:T(8,128)} %get-tuple-element.121.hat_ref, f32[896,128]{1,0:T(8,128)} %get-tuple-element.122.sums_ref, ...), custom_call_target="tpu_custom_call" | custom-call | flops 1024 | bytes 1024 | tf_op jit(solution)/shard_map/grad_in_finish/pallas_call | solution.py:518
  210.1 2.4 collective-permute-start.11
  212.5 0.7 collective-permute-start.10
  213.3 1.3 collective-permute-start.9
  214.6 2.8 %add_convert_fusion.1 = bf16[896,512]{1,0:T(8,128)(2,1)} fusion(f32[896,512]{1,0:T(8,128)S(1)} %get-tuple-element.112, bf16[896,512]{1,0:T(8,128)(2,1)} %collective-permute-done.5, bf16[896,512]{1,0:T(8,128)(2,1)} %tokens_ref.3, f32[512]{0:T(512)S(1)} %copy-done.21), kind=kLoop, calls=%fused_computation.2 | loop fusion | flops 2752512 | bytes 4589568 | tf_op jit(solution)/shard_map/convert_element_type | solution.py:875
  217.4 0.2 collective-permute-done.10
  217.7 0.6 slice.62
  218.3 0.6 slice.52
  218.9 0.6 fusion.2
  219.5 19.0 %all-gather.2.cloned.1.call-done = bf16[6144,1024]{1,0:T(8,128)(2,1)} async-done(((bf16[384,1024]{1,0:T(8,128)(2,1)}), bf16[6144,1024]{1,0:T(8,128)(2,1)}) %all-gather.2.cloned.1.call-update) | async-done | bytes 12582928 | tf_op jit(solution)/shard_map/all_gather | solution.py:701
  238.5 12.7 %spread.1 = (f32[2048,1024]{1,0:T(8,128)}, f32[1024,2048]{1,0:T(8,128)}, f32[1024,1536]{1,0:T(8,128)}, f32[512,1024]{1,0:T(8,128)}) custom-call(bf16[16,384,1024]{2,1,0:T(8,128)(2,1)} %bitcast.28, bf16[16,3,128,1024]{3,2,1,0:T(8,128)(2,1)} %bitcast.29, bf16[16,3,128,1024]{3,2,1,0:T(8,128)(2,1)} %bitcast.30), custom_call_target="tpu_custom_call" | custom-call | flops 1024 | bytes 1024 | tf_op jit(solution)/shard_map/spread/pallas_call | solution.py:321
  (55 shorter events, 0.2 us)
Async XLA Ops:
  7.2 29.9 %copy-start.15 = (f32[2048]{0:T(1024)S(1)}, f32[2048]{0:T(1024)}, u32[]{:S(2)}) copy-start(f32[2048]{0:T(1024)} %param.20) | copy-start | bytes 24580
  7.2 123.2 %reduce-scatter.3.cloned.1.call-start = ((), (), s32[]{:S(2)}) async-start(), calls=%async_computation.2 | async-start | bytes 8912896 | tf_op jit(solution)/shard_map/reduce_scatter | solution.py:687
  7.2 24.4 %collective-permute-start = (bf16[896,512]{1,0:T(8,128)(2,1)}, bf16[896,512]{1,0:T(8,128)(2,1)S(1)}, u32[]{:S(2)}, u32[]{:S(2)}) collective-permute-start(bf16[896,512]{1,0:T(8,128)(2,1)} %tokens_ref.3), channel_id=1, source_target_pairs={{0,1},{1,0},{2,3},{3,2},{4,5},{5,4},{6,7},{7,6},{8,9},{9,8},{10,11... | collective-permute-start | bytes 2752520 | tf_op jit(solution)/shard_map/ppermute | solution.py:26
  10.2 40.2 %collective-permute-start.1 = (bf16[896,512]{1,0:T(8,128)(2,1)}, bf16[896,512]{1,0:T(8,128)(2,1)S(1)}, u32[]{:S(2)}, u32[]{:S(2)}) collective-permute-start(bf16[896,512]{1,0:T(8,128)(2,1)} %cotangent_ref.1), channel_id=1, source_target_pairs={{0,1},{1,0},{2,3},{3,2},{4,5},{5,4},{6,7},{7,6},{8,9},{9,8},{10,11... | collective-permute-start | bytes 2752520 | tf_op jit(solution)/shard_map/ppermute | solution.py:26
  31.6 0.9 copy-start.17
  37.1 1.5 copy-start.1
  38.6 11.8 %copy-start.7 = (bf16[896,512]{1,0:T(8,128)(2,1)S(1)}, bf16[896,512]{1,0:T(8,128)(2,1)}, u32[]{:S(2)}) copy-start(bf16[896,512]{1,0:T(8,128)(2,1)} %cotangent_ref.1) | copy-start | bytes 2752516
  47.4 11.5 %copy-start.3 = (bf16[896,2048]{1,0:T(8,128)(2,1)}, bf16[896,2048]{1,0:T(8,128)(2,1)S(1)}, u32[]{:S(2)}) copy-start(bf16[896,2048]{1,0:T(8,128)(2,1)S(1)} %get-tuple-element.109.hidden_ref) | copy-start | bytes 11010052
  50.5 8.4 %copy-start.2 = (bf16[896,1024]{1,0:T(8,128)(2,1)S(1)}, bf16[896,1024]{1,0:T(8,128)(2,1)}, u32[]{:S(2)}) copy-start(bf16[896,1024]{1,0:T(8,128)(2,1)} %get-tuple-element.89.normed_ref) | copy-start | bytes 5505028
  71.2 1.2 copy-start.13
  71.2 95.6 %reduce-scatter.5.cloned.1.call-start = ((), (), s32[]{:S(2)}) async-start(), calls=%async_computation.3 | async-start | bytes 2359296 | tf_op jit(solution)/shard_map/reduce_scatter | solution.py:695
  72.4 2.9 %copy-start.16 = (bf16[1024,1536]{1,0:T(8,128)(2,1)S(1)}, bf16[1024,1536]{1,0:T(8,128)(2,1)}, u32[]{:S(2)}) copy-start(bf16[1024,1536]{1,0:T(8,128)(2,1)} %w_qkv_ref) | copy-start | bytes 9437188
  78.9 25.7 %copy-start.12 = (bf16[896,1024]{1,0:T(8,128)(2,1)S(1)}, bf16[896,1024]{1,0:T(8,128)(2,1)}, u32[]{:S(2)}) copy-start(bf16[896,1024]{1,0:T(8,128)(2,1)} %get-tuple-element.90.piece_ref) | copy-start | bytes 5505028
  104.6 6.2 %copy-start.5 = (bf16[896,1536]{1,0:T(8,128)(2,1)}, bf16[896,1536]{1,0:T(8,128)(2,1)S(1)}, u32[]{:S(2)}) copy-start(bf16[896,1536]{1,0:T(8,128)(2,1)S(1)} %get-tuple-element.105.grad_joined_ref.refs_0_) | copy-start | bytes 8257540
  104.6 6.2 %copy-start.8 = (bf16[512,896]{1,0:T(8,128)(2,1)}, bf16[512,896]{1,0:T(8,128)(2,1)S(1)}, u32[]{:S(2)}) copy-start(bf16[512,896]{1,0:T(8,128)(2,1)S(1)} %get-tuple-element.111.attended_ref.refs_0_) | copy-start | bytes 2752516
  112.7 4.6 %collective-permute-start.2 = (bf16[2,2,2,1,128,1024]{5,4,3,2,1,0:T(8,128)(2,1)S(1)}, bf16[2,2,2,1,128,1024]{5,4,3,2,1,0:T(8,128)(2,1)}, u32[]{:S(2)}, u32[]{:S(2)}) collective-permute-start(bf16[2,2,2,1,128,1024]{5,4,3,2,1,0:T(8,128)(2,1)S(1)} %constant_dynamic-slice_fusion), channel_id=1, source_target_pairs={{0,2},{2,0},{4,6},{6,4},{8,10},{10,8},{12,14},{14,12},{16,18},{18,... | collective-permute-start | bytes 6291464 | tf_op jit(solution)/shard_map/ppermute | solution.py:705
  117.4 13.1 %copy-start.6 = (bf16[896,1536]{1,0:T(8,128)(2,1)S(1)}, bf16[896,1536]{1,0:T(8,128)(2,1)}, u32[]{:S(2)}) copy-start(bf16[896,1536]{1,0:T(8,128)(2,1)} %copy-done.5) | copy-start | bytes 8257540
  130.4 108.1 %all-gather.2.cloned.1.call-start = ((), (), s32[]{:S(2)}) async-start(), calls=%async_computation.4 | async-start | bytes 13369344 | tf_op jit(solution)/shard_map/all_gather | solution.py:701
  130.4 2.0 copy-start.10
  132.5 11.4 %copy-start = (bf16[2048,1024]{1,0:T(8,128)(2,1)S(1)}, bf16[2048,1024]{1,0:T(8,128)(2,1)}, u32[]{:S(2)}) copy-start(bf16[2048,1024]{1,0:T(8,128)(2,1)} %w_down_ref) | copy-start | bytes 12582916
  132.5 11.4 %copy-start.4 = (bf16[896,2048]{1,0:T(8,128)(2,1)S(1)}, bf16[896,2048]{1,0:T(8,128)(2,1)}, u32[]{:S(2)}) copy-start(bf16[896,2048]{1,0:T(8,128)(2,1)} %copy-done.3) | copy-start | bytes 11010052
  132.5 11.4 %copy-start.9 = (bf16[512,896]{1,0:T(8,128)(2,1)S(1)}, bf16[512,896]{1,0:T(8,128)(2,1)}, u32[]{:S(2)}) copy-start(bf16[512,896]{1,0:T(8,128)(2,1)} %copy-done.8) | copy-start | bytes 2752516
  132.5 11.4 %copy-start.14 = (bf16[512,1024]{1,0:T(8,128)(2,1)S(1)}, bf16[512,1024]{1,0:T(8,128)(2,1)}, u32[]{:S(2)}) copy-start(bf16[512,1024]{1,0:T(8,128)(2,1)} %w_out_ref) | copy-start | bytes 3145732
  142.2 7.4 %copy-start.11 = (f32[896,512]{1,0:T(8,128)}, f32[896,512]{1,0:T(8,128)S(1)}, u32[]{:S(2)}) copy-start(f32[896,512]{1,0:T(8,128)S(1)} %get-tuple-element.114.kept_ref) | copy-start | bytes 5505028
  142.2 7.4 %copy-start.18 = (bf16[256,1024]{1,0:T(8,128)(2,1)S(1)}, bf16[256,1024]{1,0:T(8,128)(2,1)}, u32[]{:S(2)}) copy-start(bf16[256,1024]{1,0:T(8,128)(2,1)} %reduce-scatter.3.cloned.1.call-done) | copy-start | bytes 1572868
  142.2 23.2 %collective-permute-start.3 = (bf16[896,512]{1,0:T(8,128)(2,1)S(1)}, bf16[896,512]{1,0:T(8,128)(2,1)}, u32[]{:S(2)}, u32[]{:S(2)}) collective-permute-start(bf16[896,512]{1,0:T(8,128)(2,1)S(1)} %get-tuple-element.106), channel_id=1, source_target_pairs={{0,1},{1,0},{2,3},{3,2},{4,5},{5,4},{6,7},{7,6},{8,9},{9,8},{10,11... | collective-permute-start | bytes 2752520 | tf_op jit(solution)/shard_map/ppermute | solution.py:26
  168.8 41.3 %collective-permute-start.5 = (bf16[896,512]{1,0:T(8,128)(2,1)S(1)}, bf16[896,512]{1,0:T(8,128)(2,1)}, u32[]{:S(2)}, u32[]{:S(2)}) collective-permute-start(bf16[896,512]{1,0:T(8,128)(2,1)S(1)} %get-tuple-element.115), channel_id=1, source_target_pairs={{0,1},{1,0},{2,3},{3,2},{4,5},{5,4},{6,7},{7,6},{8,9},{9,8},{10,11... | collective-permute-start | bytes 2752520 | tf_op jit(solution)/shard_map/ppermute | solution.py:26
  175.1 24.9 %collective-permute-start.4 = (f32[2,960]{0,1:T(8,128)S(1)}, f32[2,960]{0,1:T(8,128)S(1)}, u32[]{:S(2)}, u32[]{:S(2)}) collective-permute-start(f32[2,960]{0,1:T(8,128)S(1)} %pad_maximum_fusion), channel_id=1, source_target_pairs={{0,1},{1,0},{2,3},{3,2},{4,5},{5,4},{6,7},{7,6},{8,9},{9,8},{10,11... | collective-permute-start | bytes 23048 | tf_op jit(solution)/shard_map/ppermute | solution.py:26
  200.1 0.8 copy-start.19
  201.7 8.4 %collective-permute-start.8 = (f32[3200]{0:T(1024)S(1)}, f32[3200]{0:T(1024)S(1)}, u32[]{:S(2)}, u32[]{:S(2)}) collective-permute-start(f32[3200]{0:T(1024)S(1)} %pad_maximum_fusion.1), channel_id=1, source_target_pairs={{0,6},{2,4},{4,2},{6,0},{8,14},{10,12},{12,10},{14,8},{16,22},{18,... | collective-permute-start | bytes 38408 | tf_op jit(solution)/shard_map/ppermute | solution.py:705
  201.7 8.4 %collective-permute-start.7 = (f32[3200]{0:T(1024)S(1)}, f32[3200]{0:T(1024)S(1)}, u32[]{:S(2)}, u32[]{:S(2)}) collective-permute-start(f32[3200]{0:T(1024)S(1)} %pad_maximum_fusion.1), channel_id=1, source_target_pairs={{0,4},{2,6},{4,0},{6,2},{8,12},{10,14},{12,8},{14,10},{16,20},{18,... | collective-permute-start | bytes 38408 | tf_op jit(solution)/shard_map/ppermute | solution.py:705
  202.1 8.0 %collective-permute-start.6 = (f32[3200]{0:T(1024)S(1)}, f32[3200]{0:T(1024)S(1)}, u32[]{:S(2)}, u32[]{:S(2)}) collective-permute-start(f32[3200]{0:T(1024)S(1)} %pad_maximum_fusion.1), channel_id=1, source_target_pairs={{0,2},{2,0},{4,6},{6,4},{8,10},{10,8},{12,14},{14,12},{16,18},{18,... | collective-permute-start | bytes 38408 | tf_op jit(solution)/shard_map/ppermute | solution.py:705
  205.4 4.7 %copy-start.20 = (f32[1,512]{1,0:T(1,128)S(1)}, f32[1,512]{1,0:T(1,128)}, u32[]{:S(2)}) copy-start(f32[1,512]{1,0:T(1,128)} %get-tuple-element.126) | copy-start | bytes 6148
  205.4 9.2 %copy-start.21 = (f32[512]{0:T(512)S(1)}, f32[512]{0:T(512)}, u32[]{:S(2)}) copy-start(f32[512]{0:T(512)} %param.22) | copy-start | bytes 6148
  210.1 7.3 %collective-permute-start.11 = (f32[3200]{0:T(1024)S(1)}, f32[3200]{0:T(1024)S(1)}, u32[]{:S(2)}, u32[]{:S(2)}) collective-permute-start(f32[3200]{0:T(1024)S(1)} %add_add_fusion.1), channel_id=1, source_target_pairs={{0,24},{2,26},{4,28},{6,30},{8,16},{10,18},{12,20},{14,22},{16,8},... | collective-permute-start | bytes 38408 | tf_op jit(solution)/shard_map/ppermute | solution.py:705
  212.5 5.1 %collective-permute-start.10 = (f32[3200]{0:T(1024)S(1)}, f32[3200]{0:T(1024)S(1)}, u32[]{:S(2)}, u32[]{:S(2)}) collective-permute-start(f32[3200]{0:T(1024)S(1)} %add_add_fusion.1), channel_id=1, source_target_pairs={{0,16},{2,18},{4,20},{6,22},{8,24},{10,26},{12,28},{14,30},{16,0},... | collective-permute-start | bytes 38408 | tf_op jit(solution)/shard_map/ppermute | solution.py:705
  213.3 4.4 %collective-permute-start.9 = (f32[3200]{0:T(1024)S(1)}, f32[3200]{0:T(1024)S(1)}, u32[]{:S(2)}, u32[]{:S(2)}) collective-permute-start(f32[3200]{0:T(1024)S(1)} %add_add_fusion.1), channel_id=1, source_target_pairs={{0,8},{2,10},{4,12},{6,14},{8,0},{10,2},{12,4},{14,6},{16,24},{18,... | collective-permute-start | bytes 38408 | tf_op jit(solution)/shard_map/ppermute | solution.py:705
Sparse Core Ops, SparseCore 0:
  71.3 58.9 reduce-scatter.2
  133.2 33.5 reduce-scatter.4
  169.0 69.4 all-gather.1

commit v3 on v2

--- a/solution.py
+++ b/solution.py
@@ -184,7 +184,7 @@
         compiler_params=pltpu.CompilerParams(vmem_limit_bytes=20 * MIB),
         cost_estimate=SHORT,
         name="mlp_slope",
-    )(side, mine, other, streamed(w_down), slope)
+    )(side, mine, other, w_down, slope)
 
 
 def first_dims(left, right):

time: 259 us -> 257 us (level)
    unnamed x44 -> x46, local copies, waits for them, and re-layouts: 6.32 us -> 6.32 us
where the time goes in v3:
time: 257 us; the launch traced here: 256 us
  Pallas kernels  101 us (39%)
  waiting for transfers between devices  89.3 us (35%)
  local copies, waits for them, and re-layouts  18.3 us (7%)
  between operations  14.1 us (5%)
  other arithmetic  14 us (5%)
  starting transfers between devices  13.2 us (5%)
  matrix products  6.51 us (3%)
    ppermute x5, waiting for transfers between devices, swap(): return lax.ppermute(values, axis, [(0, 1), (1, 0)])  55.9 us
    pallas_call x1, Pallas kernels, attention(): pl.pallas_call(functools.partial(attention_body, rows, tiles, len(joined_...  25.6 us
    all_gather x1, waiting for transfers between devices, ring_gather(): lax.all_gather(own, 'batch', axis=0, tiled=True, axis_index_groups=[ring_...  18.9 us
    pallas_call x1, Pallas kernels, spread(): pl.pallas_call(spread_body, grid=(steps,), in_specs=[pl.BlockSpec((n // s...  12.7 us
    pallas_call x1, Pallas kernels, mlp_weights(): pl.pallas_call(functools.partial(mlp_weights_body, down), grid=(down + ha...  12.3 us
    pallas_call x1, Pallas kernels, grad_in_terms(): pl.pallas_call(functools.partial(grad_in_body, len(grad_joined)), grid_sp...  9.71 us
    pallas_call x1, Pallas kernels, mlp_forward(): pl.pallas_call(mlp_body, grid=(units // block,), in_specs=[pl.BlockSpec((...  8.83 us
    reduce_scatter x1, waiting for transfers between devices, ring_scatter(): lax.psum_scatter(values, 'batch', scatter_dimension=0, tiled=True, axis_i...  8.41 us
  transfers between devices with their start and end apart: 15, of which 9 were waited for; matrix products, arithmetic and copies ran while one was open for 12% of the time, Pallas kernels for 27%

profile of v3, /device:TPU:0, one launch (start us, length us, event | category | flops | bytes accessed | tf_op | source)
XLA Modules:
  0.0 256.1 jit_solution(4866907768239454339)
XLA Ops:
  7.2 0.0 reduce-scatter.3.cloned.1.call-start
  7.2 3.0 %collective-permute-start = (bf16[896,512]{1,0:T(8,128)(2,1)}, bf16[896,512]{1,0:T(8,128)(2,1)S(1)}, u32[]{:S(2)}, u32[]{:S(2)}) collective-permute-start(bf16[896,512]{1,0:T(8,128)(2,1)} %tokens_ref.3), channel_id=1, source_target_pairs={{0,1},{1,0},{2,3},{3,2},{4,5},{5,4},{6,7},{7,6},{8,9},{9,8},{10,11... | collective-permute-start | bytes 2752520 | tf_op jit(solution)/shard_map/ppermute | solution.py:26
  10.2 0.1 collective-permute-start.1
  10.3 0.8 reshape.151
  11.1 1.4 fusion.3
  12.5 1.4 convert_reduce_fusion
  13.8 0.7 broadcast_compare_fusion
  14.5 3.3 %select_select_fusion = s32[896]{0:T(1024)S(1)} fusion(pred[896]{0:T(1024)(128)(4,1)} %constant.158, pred[896]{0:T(1024)(128)(4,1)} %constant.159, pred[896]{0:T(1024)(128)(4,1)} %constant.160, s32[]{:T(128)} %bitcast.4, s32[]{:T(128)} %bitcast.1, s32[]{:T(128)} %bitcast.2, s32[]{:T(128)} %bitcast.3), kind=kLoop, calls=%fused_computation.17 | loop fusion | flops 2688 | bytes 6288 | tf_op jit(solution)/shard_map/jit(_take)/gather | solution.py:805
  17.8 0.1 select_convert_fusion
  17.9 13.7 %collective-permute-done.other_ref = bf16[896,512]{1,0:T(8,128)(2,1)S(1)} collective-permute-done((bf16[896,512]{1,0:T(8,128)(2,1)}, bf16[896,512]{1,0:T(8,128)(2,1)S(1)}, u32[]{:S(2)}, u32[]{:S(2)}) %collective-permute-start) | collective-permute-done | bytes 917536 | tf_op jit(solution)/shard_map/ppermute | solution.py:26
  31.6 0.9 copy-done.18
  32.6 4.6 %input_norm.1 = (bf16[896,1024]{1,0:T(8,128)(2,1)}, f32[896,128]{1,0:T(8,128)}) custom-call(s32[1]{0:T(128)} %bitcast.side_ref, bf16[896,512]{1,0:T(8,128)(2,1)} %tokens_ref.3, bf16[896,512]{1,0:T(8,128)(2,1)} %copy-done.18, f32[1,1024]{1,0:T(1,128)} %bitcast.34), custom_call_target="tpu_custom_call" | custom-call | flops 1024 | bytes 1024 | tf_op jit(solution)/shard_map/input_norm/pallas_call | solution.py:102
  37.1 1.5 copy-done.2
  38.6 8.8 %mlp_forward.1 = (bf16[896,2048]{1,0:T(8,128)(2,1)S(1)}, bf16[896,2048]{1,0:T(8,128)(2,1)S(1)}) custom-call(bf16[896,1024]{1,0:T(8,128)(2,1)S(1)} %copy-done.2, bf16[1024,2048]{1,0:T(8,128)(2,1)} %w_up_ref, f32[1,2048]{1,0:T(1,128)S(1)} %bitcast.27), custom_call_target="tpu_custom_call" | custom-call | flops 1024 | bytes 1024 | tf_op jit(solution)/shard_map/mlp_forward/pallas_call | solution.py:53
  47.5 3.0 %collective-permute-done.1.other_ref = bf16[896,512]{1,0:T(8,128)(2,1)S(1)} collective-permute-done((bf16[896,512]{1,0:T(8,128)(2,1)}, bf16[896,512]{1,0:T(8,128)(2,1)S(1)}, u32[]{:S(2)}, u32[]{:S(2)}) %collective-permute-start.1) | collective-permute-done | bytes 917536 | tf_op jit(solution)/shard_map/ppermute | solution.py:26
  50.5 6.8 %mlp_slope.1 = (bf16[896,2048]{1,0:T(8,128)(2,1)S(1)}, f32[1,2048]{1,0:T(1,128)S(1)}, bf16[896,1024]{1,0:T(8,128)(2,1)S(1)}, bf16[896,2048]{1,0:T(8,128)(2,1)}, bf16[896,1024]{1,0:T(8,128)(2,1)}) custom-call(s32[1]{0:T(128)} %bitcast.side_ref, bf16[896,512]{1,0:T(8,128)(2,1)S(1)} %copy-done.8, bf16[896,512]{1,0:T(8,128)(2,1)S(1)} %collective-permute-done.1.other_ref, ...), custom_call_target="tpu_custom_call" | custom-call | flops 1024 | bytes 1024 | tf_op jit(solution)/shard_map/mlp_slope/pallas_call | solution.py:158
  57.3 12.3 %mlp_weights.1 = bf16[4096,1024]{1,0:T(8,128)(2,1)} custom-call(bf16[896,2048]{1,0:T(8,128)(2,1)S(1)} %get-tuple-element.109.hidden_ref, bf16[896,1024]{1,0:T(8,128)(2,1)S(1)} %get-tuple-element.86.piece_ref, bf16[896,1024]{1,0:T(8,128)(2,1)S(1)} %copy-done.3, bf16[896,2048]{1,0:T(8,128)(2,1)S(1)} %get-tuple-element.87.grad_pre_ref), custom_call_target="tpu_custom_call" | custom-call | flops 1024 | bytes 1024 | tf_op jit(solution)/shard_map/mlp_weights/pallas_call | solution.py:223
  69.6 0.0 reduce-scatter.5.cloned.1.call-start
  69.7 0.1 copy.43.refs_2_
  69.8 1.0 copy-done.14
  70.8 2.9 %fusion.refs_1_ = bf16[512,896]{1,0:T(8,128)(2,1)S(1)} fusion(bf16[896,1024]{1,0:T(8,128)(2,1)} %get-tuple-element.90.piece_ref, bf16[512,1024]{1,0:T(8,128)(2,1)S(1)} %copy-done.14), kind=kOutput, calls=%fused_computation.5 | convolution fusion | flops 939982848 | bytes 3801088 | tf_op jit(solution)/shard_map/dot_general | solution.py:20
  73.8 3.6 %convolution_bitcast_fusion.refs_0_ = f32[1536,896]{1,0:T(8,128)S(1)} fusion(bf16[896,1024]{1,0:T(8,128)(2,1)S(1)} %copy-done.3, bf16[1024,1536]{1,0:T(8,128)(2,1)S(1)} %copy-done.17), kind=kOutput, calls=%fused_computation.1 | convolution fusion | flops 2818572288 | bytes 10485760 | tf_op jit(solution)/shard_map/dot_general | solution.py:20
  77.4 25.6 %attention_both.1 = (bf16[512,896]{1,0:T(8,128)(2,1)S(1)}, bf16[896,1536]{1,0:T(8,128)(2,1)S(1)}, f32[128,128]{1,0:T(8,128)S(1)}) custom-call(f32[1536,896]{1,0:T(8,128)S(1)} %convolution_bitcast_fusion.refs_0_, bf16[512,896]{1,0:T(8,128)(2,1)S(1)} %fusion.refs_1_, f32[128,1]{1,0:T(8,128)S(1)} %copy.43.refs_2_, ...), custom_call_target="tpu_custom_call" | custom-call | flops 1024 | bytes 1024 | tf_op jit(solution)/shard_map/attention_both/pallas_call | solution.py:648
  103.0 6.2 %heads_weights.1 = bf16[2048,1024]{1,0:T(8,128)(2,1)} custom-call(bf16[896,1024]{1,0:T(8,128)(2,1)S(1)} %copy-done.3, bf16[896,1024]{1,0:T(8,128)(2,1)S(1)} %copy-done.13, bf16[896,1536]{1,0:T(8,128)(2,1)S(1)} %get-tuple-element.105.grad_joined_ref.refs_0_, bf16[512,896]{1,0:T(8,128)(2,1)S(1)} %get-tuple-element.111.attended_ref.refs_0_), custom_call_target="tpu_custom_call" | custom-call | flops 1024 | bytes 1024 | tf_op jit(solution)/shard_map/heads_weights/pallas_call | solution.py:267
  109.3 1.9 constant_dynamic-slice_fusion
  111.2 0.1 collective-permute-start.2
  111.3 4.3 %collective-permute-done.2 = bf16[2,2,2,1,128,1024]{5,4,3,2,1,0:T(8,128)(2,1)} collective-permute-done((bf16[2,2,2,1,128,1024]{5,4,3,2,1,0:T(8,128)(2,1)S(1)}, bf16[2,2,2,1,128,1024]{5,4,3,2,1,0:T(8,128)(2,1)}, u32[]{:S(2)}, u32[]{:S(2)}) %collective-permute-start.2) | collective-permute-done | bytes 2097184 | tf_op jit(solution)/shard_map/ppermute | solution.py:705
  115.5 4.9 %add_convert_fusion = bf16[2,2,2,1,128,1024]{5,4,3,2,1,0:T(8,128)(2,1)} fusion(bf16[2,2,2,1,128,1024]{5,4,3,2,1,0:T(8,128)(2,1)} %collective-permute-done.2, bf16[2,2,2,2,128,1024]{5,4,3,2,1,0:T(8,128)(2,1)} %bitcast.32, s32[]{:T(128)S(6)} %select_n.57), kind=kLoop, calls=%fused_computation | loop fusion | flops 4194304 | bytes 6291460 | tf_op jit(solution)/shard_map/convert_element_type | solution.py:713
  120.4 8.4 %reduce-scatter.3.cloned.1.call-done = bf16[256,1024]{1,0:T(8,128)(2,1)} async-done(((bf16[4096,1024]{1,0:T(8,128)(2,1)}), bf16[256,1024]{1,0:T(8,128)(2,1)}) %reduce-scatter.3.cloned.1.call-update) | async-done | bytes 524304 | tf_op jit(solution)/shard_map/reduce_scatter | solution.py:687
  128.8 0.0 all-gather.2.cloned.1.call-start
  128.9 2.0 copy-done.11
  131.0 9.7 %grad_in_terms.1 = (bf16[896,512]{1,0:T(8,128)(2,1)S(1)}, f32[896,512]{1,0:T(8,128)S(1)}) custom-call(s32[1]{0:T(128)} %bitcast.side_ref, bf16[1024,1536]{1,0:T(8,128)(2,1)} %w_qkv_ref, bf16[896,2048]{1,0:T(8,128)(2,1)S(1)} %copy-done.11, bf16[1024,2048]{1,0:T(8,128)(2,1)} %w_up_ref, bf16[896,1536]{1,0:T(8,128)(2,1)S(1)} %copy-done.7), custom_call_target="tpu_custom_call" | custom-call | flops 1024 | bytes 1024 | tf_op jit(solution)/shard_map/grad_in_terms/pallas_call | solution.py:430
  140.7 1.6 collective-permute-start.3
  142.3 5.7 %output_terms.1 = (bf16[896,512]{1,0:T(8,128)(2,1)S(1)}, f32[896,512]{1,0:T(8,128)S(1)}) custom-call(s32[1]{0:T(128)} %bitcast.side_ref, bf16[512,1024]{1,0:T(8,128)(2,1)S(1)} %copy-done.15, bf16[896,2048]{1,0:T(8,128)(2,1)S(1)} %copy-done.5, bf16[2048,1024]{1,0:T(8,128)(2,1)S(1)} %copy-done.1, bf16[512,896]{1,0:T(8,128)(2,1)S(1)} %copy-done.10), custom_call_target="tpu_custom_call" | custom-call | flops 1024 | bytes 1024 | tf_op jit(solution)/shard_map/output_terms/pallas_call | solution.py:375
  148.1 1.0 dynamic_update_slice.6
  149.0 14.8 %collective-permute-done.3.arrived_ref = bf16[896,512]{1,0:T(8,128)(2,1)} collective-permute-done((bf16[896,512]{1,0:T(8,128)(2,1)S(1)}, bf16[896,512]{1,0:T(8,128)(2,1)}, u32[]{:S(2)}, u32[]{:S(2)}) %collective-permute-start.3) | collective-permute-done | bytes 917536 | tf_op jit(solution)/shard_map/ppermute | solution.py:26
  163.8 1.4 reduce-scatter.5.cloned.1.call-done
  165.2 1.7 constant_dynamic-update-slice_fusion
  166.9 0.1 reduce_sum.19
  167.0 0.1 reshape.156
  167.1 0.1 copy.44
  167.2 1.5 collective-permute-start.5
  168.7 3.6 %grad_in_hat.1 = (f32[896,512]{1,0:T(8,128)}, f32[896,128]{1,0:T(8,128)}, f32[1,512]{1,0:T(1,128)}) custom-call(s32[1]{0:T(128)} %bitcast.side_ref, f32[896,512]{1,0:T(8,128)} %copy-done.12, bf16[896,512]{1,0:T(8,128)(2,1)} %collective-permute-done.3.arrived_ref, bf16[896,512]{1,0:T(8,128)(2,1)} %tokens_ref.3, f32[896,128]{1,0:T(8,128)} %get-tuple-element.113.stats_ref, ...), custom_call_target="tpu_custom_call" | custom-call | flops 1024 | bytes 1024 | tf_op jit(solution)/shard_map/grad_in_hat/pallas_call | solution.py:481
  172.3 1.2 slice_bitcast_fusion.1
  173.5 0.5 collective-permute-start.4
  174.0 24.5 %collective-permute-done.4 = f32[2,960]{0,1:T(8,128)S(1)} collective-permute-done((f32[2,960]{0,1:T(8,128)S(1)}, f32[2,960]{0,1:T(8,128)S(1)}, u32[]{:S(2)}, u32[]{:S(2)}) %collective-permute-start.4) | collective-permute-done | bytes 7712 | tf_op jit(solution)/shard_map/ppermute | solution.py:26
  198.5 0.8 copy-done.20
  199.2 0.1 copy.46
  199.3 0.1 reshape.157
  199.4 0.7 pad_maximum_fusion.1
  200.1 0.1 collective-permute-start.7
  200.2 1.8 collective-permute-start.6
  202.0 1.8 slice_bitcast_fusion.other_ref
  203.8 4.7 %grad_in_finish.1 = bf16[896,512]{1,0:T(8,128)(2,1)} custom-call(bf16[896,512]{1,0:T(8,128)(2,1)} %cotangent_ref.1, bf16[896,512]{1,0:T(8,128)(2,1)} %tokens_ref.3, f32[896,128]{1,0:T(8,128)} %get-tuple-element.113.stats_ref, f32[896,512]{1,0:T(8,128)} %get-tuple-element.121.hat_ref, f32[896,128]{1,0:T(8,128)} %get-tuple-element.122.sums_ref, ...), custom_call_target="tpu_custom_call" | custom-call | flops 1024 | bytes 1024 | tf_op jit(solution)/shard_map/grad_in_finish/pallas_call | solution.py:518
  208.5 2.5 collective-permute-start.11
  211.1 0.7 collective-permute-start.10
  211.8 1.2 collective-permute-start.9
  213.0 2.8 %add_convert_fusion.1 = bf16[896,512]{1,0:T(8,128)(2,1)} fusion(f32[896,512]{1,0:T(8,128)S(1)} %get-tuple-element.112, bf16[896,512]{1,0:T(8,128)(2,1)} %collective-permute-done.5, bf16[896,512]{1,0:T(8,128)(2,1)} %tokens_ref.3, f32[512]{0:T(512)S(1)} %copy-done.22), kind=kLoop, calls=%fused_computation.2 | loop fusion | flops 2752512 | bytes 4589568 | tf_op jit(solution)/shard_map/convert_element_type | solution.py:875
  215.8 0.4 collective-permute-done.10
  216.2 0.6 slice.62
  216.8 0.6 slice.52
  217.4 0.6 fusion.2
  218.0 18.9 %all-gather.2.cloned.1.call-done = bf16[6144,1024]{1,0:T(8,128)(2,1)} async-done(((bf16[384,1024]{1,0:T(8,128)(2,1)}), bf16[6144,1024]{1,0:T(8,128)(2,1)}) %all-gather.2.cloned.1.call-update) | async-done | bytes 12582928 | tf_op jit(solution)/shard_map/all_gather | solution.py:701
  236.9 12.7 %spread.1 = (f32[2048,1024]{1,0:T(8,128)}, f32[1024,2048]{1,0:T(8,128)}, f32[1024,1536]{1,0:T(8,128)}, f32[512,1024]{1,0:T(8,128)}) custom-call(bf16[16,384,1024]{2,1,0:T(8,128)(2,1)} %bitcast.28, bf16[16,3,128,1024]{3,2,1,0:T(8,128)(2,1)} %bitcast.29, bf16[16,3,128,1024]{3,2,1,0:T(8,128)(2,1)} %bitcast.30), custom_call_target="tpu_custom_call" | custom-call | flops 1024 | bytes 1024 | tf_op jit(solution)/shard_map/spread/pallas_call | solution.py:321
  (57 shorter events, 0.2 us)
Async XLA Ops:
  7.2 29.9 %copy-start.16 = (f32[2048]{0:T(1024)S(1)}, f32[2048]{0:T(1024)}, u32[]{:S(2)}) copy-start(f32[2048]{0:T(1024)} %param.20) | copy-start | bytes 24580
  7.2 121.6 %reduce-scatter.3.cloned.1.call-start = ((), (), s32[]{:S(2)}) async-start(), calls=%async_computation.2 | async-start | bytes 8912896 | tf_op jit(solution)/shard_map/reduce_scatter | solution.py:687
  7.2 24.4 %collective-permute-start = (bf16[896,512]{1,0:T(8,128)(2,1)}, bf16[896,512]{1,0:T(8,128)(2,1)S(1)}, u32[]{:S(2)}, u32[]{:S(2)}) collective-permute-start(bf16[896,512]{1,0:T(8,128)(2,1)} %tokens_ref.3), channel_id=1, source_target_pairs={{0,1},{1,0},{2,3},{3,2},{4,5},{5,4},{6,7},{7,6},{8,9},{9,8},{10,11... | collective-permute-start | bytes 2752520 | tf_op jit(solution)/shard_map/ppermute | solution.py:26
  10.2 40.2 %collective-permute-start.1 = (bf16[896,512]{1,0:T(8,128)(2,1)}, bf16[896,512]{1,0:T(8,128)(2,1)S(1)}, u32[]{:S(2)}, u32[]{:S(2)}) collective-permute-start(bf16[896,512]{1,0:T(8,128)(2,1)} %cotangent_ref.1), channel_id=1, source_target_pairs={{0,1},{1,0},{2,3},{3,2},{4,5},{5,4},{6,7},{7,6},{8,9},{9,8},{10,11... | collective-permute-start | bytes 2752520 | tf_op jit(solution)/shard_map/ppermute | solution.py:26
  31.6 0.9 copy-start.18
  37.1 1.5 copy-start.2
  38.6 11.8 %copy-start = (bf16[2048,1024]{1,0:T(8,128)(2,1)S(1)}, bf16[2048,1024]{1,0:T(8,128)(2,1)}, u32[]{:S(2)}) copy-start(bf16[2048,1024]{1,0:T(8,128)(2,1)} %w_down_ref) | copy-start | bytes 12582916
  38.6 11.8 %copy-start.8 = (bf16[896,512]{1,0:T(8,128)(2,1)S(1)}, bf16[896,512]{1,0:T(8,128)(2,1)}, u32[]{:S(2)}) copy-start(bf16[896,512]{1,0:T(8,128)(2,1)} %cotangent_ref.1) | copy-start | bytes 2752516
  47.5 9.8 %copy-start.4 = (bf16[896,2048]{1,0:T(8,128)(2,1)}, bf16[896,2048]{1,0:T(8,128)(2,1)S(1)}, u32[]{:S(2)}) copy-start(bf16[896,2048]{1,0:T(8,128)(2,1)S(1)} %get-tuple-element.109.hidden_ref) | copy-start | bytes 11010052
  50.5 6.8 %copy-start.3 = (bf16[896,1024]{1,0:T(8,128)(2,1)S(1)}, bf16[896,1024]{1,0:T(8,128)(2,1)}, u32[]{:S(2)}) copy-start(bf16[896,1024]{1,0:T(8,128)(2,1)} %get-tuple-element.89.normed_ref) | copy-start | bytes 5505028
  69.6 1.2 copy-start.14
  69.6 95.6 %reduce-scatter.5.cloned.1.call-start = ((), (), s32[]{:S(2)}) async-start(), calls=%async_computation.3 | async-start | bytes 2359296 | tf_op jit(solution)/shard_map/reduce_scatter | solution.py:695
  70.8 2.9 %copy-start.17 = (bf16[1024,1536]{1,0:T(8,128)(2,1)S(1)}, bf16[1024,1536]{1,0:T(8,128)(2,1)}, u32[]{:S(2)}) copy-start(bf16[1024,1536]{1,0:T(8,128)(2,1)} %w_qkv_ref) | copy-start | bytes 9437188
  77.4 25.7 %copy-start.13 = (bf16[896,1024]{1,0:T(8,128)(2,1)S(1)}, bf16[896,1024]{1,0:T(8,128)(2,1)}, u32[]{:S(2)}) copy-start(bf16[896,1024]{1,0:T(8,128)(2,1)} %get-tuple-element.90.piece_ref) | copy-start | bytes 5505028
  103.0 6.2 %copy-start.6 = (bf16[896,1536]{1,0:T(8,128)(2,1)}, bf16[896,1536]{1,0:T(8,128)(2,1)S(1)}, u32[]{:S(2)}) copy-start(bf16[896,1536]{1,0:T(8,128)(2,1)S(1)} %get-tuple-element.105.grad_joined_ref.refs_0_) | copy-start | bytes 8257540
  103.0 6.2 %copy-start.9 = (bf16[512,896]{1,0:T(8,128)(2,1)}, bf16[512,896]{1,0:T(8,128)(2,1)S(1)}, u32[]{:S(2)}) copy-start(bf16[512,896]{1,0:T(8,128)(2,1)S(1)} %get-tuple-element.111.attended_ref.refs_0_) | copy-start | bytes 2752516
  111.2 4.4 %collective-permute-start.2 = (bf16[2,2,2,1,128,1024]{5,4,3,2,1,0:T(8,128)(2,1)S(1)}, bf16[2,2,2,1,128,1024]{5,4,3,2,1,0:T(8,128)(2,1)}, u32[]{:S(2)}, u32[]{:S(2)}) collective-permute-start(bf16[2,2,2,1,128,1024]{5,4,3,2,1,0:T(8,128)(2,1)S(1)} %constant_dynamic-slice_fusion), channel_id=1, source_target_pairs={{0,2},{2,0},{4,6},{6,4},{8,10},{10,8},{12,14},{14,12},{16,18},{18,... | collective-permute-start | bytes 6291464 | tf_op jit(solution)/shard_map/ppermute | solution.py:705
  115.5 13.4 %copy-start.7 = (bf16[896,1536]{1,0:T(8,128)(2,1)S(1)}, bf16[896,1536]{1,0:T(8,128)(2,1)}, u32[]{:S(2)}) copy-start(bf16[896,1536]{1,0:T(8,128)(2,1)} %copy-done.6) | copy-start | bytes 8257540
  128.8 108.1 %all-gather.2.cloned.1.call-start = ((), (), s32[]{:S(2)}) async-start(), calls=%async_computation.4 | async-start | bytes 13369344 | tf_op jit(solution)/shard_map/all_gather | solution.py:701
  128.9 2.0 copy-start.11
  130.9 11.3 %copy-start.1 = (bf16[2048,1024]{1,0:T(8,128)(2,1)S(1)}, bf16[2048,1024]{1,0:T(8,128)(2,1)}, u32[]{:S(2)}) copy-start(bf16[2048,1024]{1,0:T(8,128)(2,1)} %w_down_ref) | copy-start | bytes 12582916
  130.9 11.3 %copy-start.5 = (bf16[896,2048]{1,0:T(8,128)(2,1)S(1)}, bf16[896,2048]{1,0:T(8,128)(2,1)}, u32[]{:S(2)}) copy-start(bf16[896,2048]{1,0:T(8,128)(2,1)} %copy-done.4) | copy-start | bytes 11010052
  130.9 11.3 %copy-start.10 = (bf16[512,896]{1,0:T(8,128)(2,1)S(1)}, bf16[512,896]{1,0:T(8,128)(2,1)}, u32[]{:S(2)}) copy-start(bf16[512,896]{1,0:T(8,128)(2,1)} %copy-done.9) | copy-start | bytes 2752516
  131.0 11.3 %copy-start.15 = (bf16[512,1024]{1,0:T(8,128)(2,1)S(1)}, bf16[512,1024]{1,0:T(8,128)(2,1)}, u32[]{:S(2)}) copy-start(bf16[512,1024]{1,0:T(8,128)(2,1)} %w_out_ref) | copy-start | bytes 3145732
  140.7 7.4 %copy-start.12 = (f32[896,512]{1,0:T(8,128)}, f32[896,512]{1,0:T(8,128)S(1)}, u32[]{:S(2)}) copy-start(f32[896,512]{1,0:T(8,128)S(1)} %get-tuple-element.114.kept_ref) | copy-start | bytes 5505028
  140.7 7.4 %copy-start.19 = (bf16[256,1024]{1,0:T(8,128)(2,1)S(1)}, bf16[256,1024]{1,0:T(8,128)(2,1)}, u32[]{:S(2)}) copy-start(bf16[256,1024]{1,0:T(8,128)(2,1)} %reduce-scatter.3.cloned.1.call-done) | copy-start | bytes 1572868
  140.7 23.1 %collective-permute-start.3 = (bf16[896,512]{1,0:T(8,128)(2,1)S(1)}, bf16[896,512]{1,0:T(8,128)(2,1)}, u32[]{:S(2)}, u32[]{:S(2)}) collective-permute-start(bf16[896,512]{1,0:T(8,128)(2,1)S(1)} %get-tuple-element.106), channel_id=1, source_target_pairs={{0,1},{1,0},{2,3},{3,2},{4,5},{5,4},{6,7},{7,6},{8,9},{9,8},{10,11... | collective-permute-start | bytes 2752520 | tf_op jit(solution)/shard_map/ppermute | solution.py:26
  167.2 41.3 %collective-permute-start.5 = (bf16[896,512]{1,0:T(8,128)(2,1)S(1)}, bf16[896,512]{1,0:T(8,128)(2,1)}, u32[]{:S(2)}, u32[]{:S(2)}) collective-permute-start(bf16[896,512]{1,0:T(8,128)(2,1)S(1)} %get-tuple-element.115), channel_id=1, source_target_pairs={{0,1},{1,0},{2,3},{3,2},{4,5},{5,4},{6,7},{7,6},{8,9},{9,8},{10,11... | collective-permute-start | bytes 2752520 | tf_op jit(solution)/shard_map/ppermute | solution.py:26
  173.5 24.9 %collective-permute-start.4 = (f32[2,960]{0,1:T(8,128)S(1)}, f32[2,960]{0,1:T(8,128)S(1)}, u32[]{:S(2)}, u32[]{:S(2)}) collective-permute-start(f32[2,960]{0,1:T(8,128)S(1)} %pad_maximum_fusion), channel_id=1, source_target_pairs={{0,1},{1,0},{2,3},{3,2},{4,5},{5,4},{6,7},{7,6},{8,9},{9,8},{10,11... | collective-permute-start | bytes 23048 | tf_op jit(solution)/shard_map/ppermute | solution.py:26
  198.5 0.8 copy-start.20
  200.1 8.4 %collective-permute-start.8 = (f32[3200]{0:T(1024)S(1)}, f32[3200]{0:T(1024)S(1)}, u32[]{:S(2)}, u32[]{:S(2)}) collective-permute-start(f32[3200]{0:T(1024)S(1)} %pad_maximum_fusion.1), channel_id=1, source_target_pairs={{0,6},{2,4},{4,2},{6,0},{8,14},{10,12},{12,10},{14,8},{16,22},{18,... | collective-permute-start | bytes 38408 | tf_op jit(solution)/shard_map/ppermute | solution.py:705
  200.1 8.4 %collective-permute-start.7 = (f32[3200]{0:T(1024)S(1)}, f32[3200]{0:T(1024)S(1)}, u32[]{:S(2)}, u32[]{:S(2)}) collective-permute-start(f32[3200]{0:T(1024)S(1)} %pad_maximum_fusion.1), channel_id=1, source_target_pairs={{0,4},{2,6},{4,0},{6,2},{8,12},{10,14},{12,8},{14,10},{16,20},{18,... | collective-permute-start | bytes 38408 | tf_op jit(solution)/shard_map/ppermute | solution.py:705
  200.2 8.3 %collective-permute-start.6 = (f32[3200]{0:T(1024)S(1)}, f32[3200]{0:T(1024)S(1)}, u32[]{:S(2)}, u32[]{:S(2)}) collective-permute-start(f32[3200]{0:T(1024)S(1)} %pad_maximum_fusion.1), channel_id=1, source_target_pairs={{0,2},{2,0},{4,6},{6,4},{8,10},{10,8},{12,14},{14,12},{16,18},{18,... | collective-permute-start | bytes 38408 | tf_op jit(solution)/shard_map/ppermute | solution.py:705
  203.8 4.7 %copy-start.21 = (f32[1,512]{1,0:T(1,128)S(1)}, f32[1,512]{1,0:T(1,128)}, u32[]{:S(2)}) copy-start(f32[1,512]{1,0:T(1,128)} %get-tuple-element.126) | copy-start | bytes 6148
  203.8 9.2 %copy-start.22 = (f32[512]{0:T(512)S(1)}, f32[512]{0:T(512)}, u32[]{:S(2)}) copy-start(f32[512]{0:T(512)} %param.22) | copy-start | bytes 6148
  208.5 7.3 %collective-permute-start.11 = (f32[3200]{0:T(1024)S(1)}, f32[3200]{0:T(1024)S(1)}, u32[]{:S(2)}, u32[]{:S(2)}) collective-permute-start(f32[3200]{0:T(1024)S(1)} %add_add_fusion.1), channel_id=1, source_target_pairs={{0,24},{2,26},{4,28},{6,30},{8,16},{10,18},{12,20},{14,22},{16,8},... | collective-permute-start | bytes 38408 | tf_op jit(solution)/shard_map/ppermute | solution.py:705
  211.1 5.1 %collective-permute-start.10 = (f32[3200]{0:T(1024)S(1)}, f32[3200]{0:T(1024)S(1)}, u32[]{:S(2)}, u32[]{:S(2)}) collective-permute-start(f32[3200]{0:T(1024)S(1)} %add_add_fusion.1), channel_id=1, source_target_pairs={{0,16},{2,18},{4,20},{6,22},{8,24},{10,26},{12,28},{14,30},{16,0},... | collective-permute-start | bytes 38408 | tf_op jit(solution)/shard_map/ppermute | solution.py:705
  211.8 4.4 %collective-permute-start.9 = (f32[3200]{0:T(1024)S(1)}, f32[3200]{0:T(1024)S(1)}, u32[]{:S(2)}, u32[]{:S(2)}) collective-permute-start(f32[3200]{0:T(1024)S(1)} %add_add_fusion.1), channel_id=1, source_target_pairs={{0,8},{2,10},{4,12},{6,14},{8,0},{10,2},{12,4},{14,6},{16,24},{18,... | collective-permute-start | bytes 38408 | tf_op jit(solution)/shard_map/ppermute | solution.py:705
Sparse Core Ops, SparseCore 0:
  69.7 59.0 reduce-scatter.2
  131.7 33.4 reduce-scatter.4
  167.4 69.5 all-gather.1
